TPU v7x, 32 devices: a whole 2x2x4 slice. The times are simulated.
32 devices in a mesh: seq: 8 (over y, x, core), head: 4 (over z).
Axes of the slice: x: 2, y: 2, z: 4, core: 2. Of those that a mesh axis runs over, the one named last changes fastest.
Arguments:
- inputs: bfloat16 [8, 1024, 512], P(None, ('seq', 'head')), may hold values from -8 to 8
- gain_first: float32 [512], replicated, may hold values from 0.25 to 1.75
- shift_first: float32 [512], replicated, may hold values from -3 to 3
- query_weight: bfloat16 [512, 512], replicated, may hold values from -0.25 to 0.25
- key_weight: bfloat16 [512, 512], replicated, may hold values from -0.25 to 0.25
- value_weight: bfloat16 [512, 512], replicated, may hold values from -0.25 to 0.25
- out_weight: bfloat16 [512, 512], replicated, may hold values from -1 to 1
- gain_second: float32 [512], replicated, may hold values from 0.25 to 1.75
- shift_second: float32 [512], replicated, may hold values from -3 to 3
- up_weight: bfloat16 [512, 2048], replicated, may hold values from -0.25 to 0.25
- up_bias: float32 [2048], replicated, may hold values from -3 to 3
- down_weight: bfloat16 [2048, 512], replicated, may hold values from -0.125 to 0.125
- down_bias: float32 [512], replicated, may hold values from -3 to 3
- cotangent: bfloat16 [8, 1024, 512], P(None, ('seq', 'head')), may hold values from -6 to 6
Outputs:
- layer_out: bfloat16 [8, 1024, 512], P(None, ('seq', 'head'))
- input_grad: bfloat16 [8, 1024, 512], P(None, ('seq', 'head'))
- gain_first_grad: float32 [512], P('seq')
- shift_first_grad: float32 [512], P('seq')
- query_grad: float32 [512, 512], P('seq', 'head')
- key_grad: float32 [512, 512], P('seq', 'head')
- value_grad: float32 [512, 512], P('seq', 'head')
- out_weight_grad: float32 [512, 512], P('seq', 'head')
- gain_second_grad: float32 [512], P('seq')
- shift_second_grad: float32 [512], P('seq')
- up_grad: float32 [512, 2048], P('seq', 'head')
- up_bias_grad: float32 [2048], P('seq')
- down_grad: float32 [2048, 512], P('seq', 'head')
- down_bias_grad: float32 [512], P('seq')
All inputs are finite; a program needn't handle non-finite values.
Results may differ from a plain program's by a relative error of at most 0.009.
Values may be sent and summed in bfloat16 or wider, within the bound.
A program may use at most 192 MiB of HBM per device.

v0:
```python
import jax
import jax.numpy as jnp
from jax import lax
from jax.sharding import PartitionSpec as P

H = 8
DH = 64
BLOCK = 16
LOC = 128
ROWS_MB = 2
MICRO = 4


EPSILON = 1e-05


def in_blocks(value, dim, length):
    before, after = (value.shape[:dim], value.shape[dim + 1 :])
    return jnp.moveaxis(value.reshape(*before, length, -1, *after), dim, 0)


def sum_at_owner(value, axis, dim):
    parts = in_blocks(value, dim, lax.axis_size(axis))
    arrived = lax.all_to_all(parts, axis, split_axis=0, concat_axis=0, tiled=True)
    return arrived.astype(jnp.float32).sum(axis=0)


def norm_rows(values, gain, shift):
    center = values - jnp.mean(values, axis=-1, keepdims=True)
    spread = jnp.mean(center * center, axis=-1, keepdims=True)
    return center * lax.rsqrt(spread + EPSILON) * gain + shift


def exact_gelu(values):
    return jax.nn.gelu(values, approximate=False)


def halve_axis(table, axis_id):
    shape_in = table.shape
    paired = table.astype(jnp.float32).reshape(
        shape_in[:axis_id] + (shape_in[axis_id] // 2, 2) + shape_in[axis_id + 1 :]
    )
    return (jnp.sum(paired, axis=axis_id + 1) * 0.5).astype(jnp.bfloat16)


def spread_axis(grad_in, axis_id):
    return jnp.repeat(grad_in * 0.5, 2, axis=axis_id)


def flip_blocks(table):
    shape_in = table.shape
    split_view = table.reshape((shape_in[0], shape_in[1] // (2 * BLOCK), 2, BLOCK) + shape_in[2:])
    return split_view[:, :, ::-1].reshape(shape_in)


def group_scores(left, right):
    shape_in = left.shape
    groups = right.shape[1] // BLOCK
    left_view = left.reshape(shape_in[0], groups, shape_in[1] // groups, shape_in[2], shape_in[3])
    right_view = right.reshape(shape_in[0], groups, BLOCK, shape_in[2], shape_in[3])
    product = jnp.einsum(
        "rbmhd,rbkhd->rbmhk", left_view, right_view, preferred_element_type=jnp.float32
    )
    return product.reshape(shape_in[0], shape_in[1], shape_in[2], BLOCK)


def group_values(weights, right):
    shape_in = weights.shape
    groups = right.shape[1] // BLOCK
    left_view = weights.reshape(shape_in[0], groups, shape_in[1] // groups, shape_in[2], BLOCK)
    right_view = right.reshape(shape_in[0], groups, BLOCK, shape_in[2], right.shape[3])
    product = jnp.einsum(
        "rbmhk,rbkhd->rbmhd", left_view, right_view, preferred_element_type=jnp.float32
    )
    return product.reshape(shape_in[0], shape_in[1], shape_in[2], right.shape[3])


def group_keys(weights, left, key_count):
    shape_in = left.shape
    groups = key_count // BLOCK
    weight_view = weights.reshape(shape_in[0], groups, shape_in[1] // groups, shape_in[2], BLOCK)
    left_view = left.reshape(shape_in[0], groups, shape_in[1] // groups, shape_in[2], shape_in[3])
    product = jnp.einsum(
        "rbmhk,rbmhd->rbkhd", weight_view, left_view, preferred_element_type=jnp.float32
    )
    return product.reshape(shape_in[0], key_count, shape_in[2], shape_in[3])


def attend_forward(queries, key_sets, value_sets, score_scale):
    scores = (
        jnp.concatenate([group_scores(queries, keyset) for keyset in key_sets], axis=-1)
        * score_scale
    )
    row_max = jnp.max(scores, axis=-1, keepdims=True)
    shifted = jnp.exp(scores - row_max)
    probability = shifted / jnp.sum(shifted, axis=-1, keepdims=True)
    weights = probability.astype(jnp.bfloat16)
    mixed = jnp.zeros(queries.shape, jnp.float32)
    for position, valueset in enumerate(value_sets):
        mixed = mixed + group_values(
            weights[..., BLOCK * position : BLOCK * (position + 1)], valueset
        )
    return (mixed.astype(jnp.bfloat16), probability, weights)


def attend_backward(grad_mixed, queries, key_sets, value_sets, probability, weights, score_scale):
    grad_prob = jnp.concatenate(
        [group_scores(grad_mixed, valueset) for valueset in value_sets], axis=-1
    )
    inner_sum = jnp.sum(probability * grad_prob, axis=-1, keepdims=True)
    grad_scores = (probability * (grad_prob - inner_sum)).astype(jnp.bfloat16)
    grad_query = jnp.zeros(queries.shape, jnp.float32)
    key_grads = []
    value_grads = []
    for position in range(len(key_sets)):
        piece_scores = grad_scores[..., BLOCK * position : BLOCK * (position + 1)]
        piece_weights = weights[..., BLOCK * position : BLOCK * (position + 1)]
        grad_query = grad_query + group_values(piece_scores, key_sets[position])
        key_grads.append(
            group_keys(piece_scores, queries, key_sets[position].shape[1]) * score_scale
        )
        value_grads.append(group_keys(piece_weights, grad_mixed, value_sets[position].shape[1]))
    return (grad_query * score_scale, key_grads, value_grads)


def pack_block(matrix, seq_count, head_count):
    row_count, col_count = matrix.shape
    blocks = matrix.reshape(seq_count, row_count // seq_count, head_count, col_count // head_count)
    return blocks.transpose(0, 2, 1, 3).reshape(row_count * head_count, col_count // head_count)


def pack_line(vector, seq_count, head_count):
    piece_len = vector.shape[0] // seq_count
    return jnp.broadcast_to(
        vector.reshape(seq_count, 1, piece_len), (seq_count, head_count, piece_len)
    ).reshape(-1)


def pack_shared(shared_raw, seq_count, head_count):
    (
        out_g,
        up_g,
        down_g,
        up_bias_g,
        down_bias_g,
        gain_one_g,
        shift_one_g,
        gain_two_g,
        shift_two_g,
    ) = shared_raw
    return (
        pack_block(out_g, seq_count, head_count),
        pack_block(up_g, seq_count, head_count),
        pack_block(down_g, seq_count, head_count),
        pack_line(up_bias_g, seq_count, head_count),
        pack_line(down_bias_g, seq_count, head_count),
        pack_line(gain_one_g, seq_count, head_count),
        pack_line(shift_one_g, seq_count, head_count),
        pack_line(gain_two_g, seq_count, head_count),
        pack_line(shift_two_g, seq_count, head_count),
    )


def body(
    inputs,
    gain_first,
    shift_first,
    query_weight,
    key_weight,
    value_weight,
    out_weight,
    gain_second,
    shift_second,
    up_weight,
    up_bias,
    down_weight,
    down_bias,
    cotangent,
):
    seq_count = lax.axis_size("seq")
    head_count = lax.axis_size("head")
    seq_index = lax.axis_index("seq")
    head_index = lax.axis_index("head")
    seq_bits = seq_count.bit_length() - 1
    local_levels = (LOC // BLOCK).bit_length() - 1
    model_width = inputs.shape[2]
    part_width = model_width // head_count
    heads_here = H // head_count
    score_scale = DH ** (-0.5)
    col_start = head_index * part_width
    query_part = lax.dynamic_slice_in_dim(query_weight, col_start, part_width, 1)
    key_part = lax.dynamic_slice_in_dim(key_weight, col_start, part_width, 1)
    value_part = lax.dynamic_slice_in_dim(value_weight, col_start, part_width, 1)
    head_total = None
    shared_total = None
    out_rows = []
    grad_rows = []
    for micro_id in range(MICRO):
        lower_row = micro_id * ROWS_MB
        x_local = inputs[lower_row : lower_row + ROWS_MB]
        grad_local = cotangent[lower_row : lower_row + ROWS_MB]
        x_gathered = lax.all_gather(x_local, "head", axis=1, tiled=True)
        normed = norm_rows(x_gathered.astype(jnp.float32), gain_first, shift_first).astype(
            jnp.bfloat16
        )
        queries = (
            jnp.dot(normed, query_part, preferred_element_type=jnp.float32)
            .astype(jnp.bfloat16)
            .reshape(ROWS_MB, LOC, heads_here, DH)
        )
        keyrows = (
            jnp.dot(normed, key_part, preferred_element_type=jnp.float32)
            .astype(jnp.bfloat16)
            .reshape(ROWS_MB, LOC, heads_here, DH)
        )
        valrows = (
            jnp.dot(normed, value_part, preferred_element_type=jnp.float32)
            .astype(jnp.bfloat16)
            .reshape(ROWS_MB, LOC, heads_here, DH)
        )
        key_sets = [keyrows]
        value_sets = [valrows]
        coarse_key, coarse_value = (keyrows, valrows)
        for level_id in range(local_levels):
            key_sets.append(flip_blocks(coarse_key))
            value_sets.append(flip_blocks(coarse_value))
            coarse_key = halve_axis(coarse_key, 1)
            coarse_value = halve_axis(coarse_value, 1)
        summary = jnp.stack([coarse_key, coarse_value]).reshape(2, ROWS_MB, BLOCK, part_width)
        remote = []
        whole_level = lax.all_gather(summary, "seq", axis=2, tiled=True)
        for bit_id in range(seq_bits):
            group_id = seq_index // 2**bit_id
            sibling = group_id + 1 - 2 * (group_id % 2)
            remote.append(lax.dynamic_slice_in_dim(whole_level, sibling * BLOCK, BLOCK, 2))
            if bit_id + 1 < seq_bits:
                whole_level = halve_axis(whole_level, 2)
        for partner in remote:
            key_sets.append(partner[0].reshape(ROWS_MB, BLOCK, heads_here, DH))
            value_sets.append(partner[1].reshape(ROWS_MB, BLOCK, heads_here, DH))
        mixed, probability, weights = attend_forward(queries, key_sets, value_sets, score_scale)
        mixed_tokens = lax.all_to_all(
            mixed.reshape(ROWS_MB, LOC, part_width), "head", split_axis=1, concat_axis=2, tiled=True
        )
        x_tokens = x_local.astype(jnp.float32)
        residual = x_tokens + jnp.dot(mixed_tokens, out_weight, preferred_element_type=jnp.float32)
        normed_two, norm_two_back = jax.vjp(norm_rows, residual, gain_second, shift_second)
        normed_two = normed_two.astype(jnp.bfloat16)
        hidden = jnp.dot(normed_two, up_weight, preferred_element_type=jnp.float32) + up_bias
        active, gelu_back = jax.vjp(exact_gelu, hidden)
        active = active.astype(jnp.bfloat16)
        result = (
            residual + jnp.dot(active, down_weight, preferred_element_type=jnp.float32) + down_bias
        )
        out_rows.append(result.astype(jnp.bfloat16))
        grad_float = grad_local.astype(jnp.float32)
        down_g = jnp.einsum("rnf,rnd->fd", active, grad_local, preferred_element_type=jnp.float32)
        down_bias_g = jnp.sum(grad_float, axis=(0, 1))
        grad_active = jnp.einsum(
            "rnd,fd->rnf", grad_local, down_weight, preferred_element_type=jnp.float32
        )
        (grad_hidden,) = gelu_back(grad_active)
        grad_hidden = grad_hidden.astype(jnp.bfloat16)
        up_g = jnp.einsum(
            "rnd,rnf->df", normed_two, grad_hidden, preferred_element_type=jnp.float32
        )
        up_bias_g = jnp.sum(grad_hidden.astype(jnp.float32), axis=(0, 1))
        grad_normed_two = jnp.einsum(
            "rnf,df->rnd", grad_hidden, up_weight, preferred_element_type=jnp.float32
        )
        grad_norm_part, gain_two_g, shift_two_g = norm_two_back(grad_normed_two)
        grad_residual = grad_float + grad_norm_part
        grad_mix = grad_residual.astype(jnp.bfloat16)
        out_g = jnp.einsum(
            "rnd,rne->de", mixed_tokens, grad_mix, preferred_element_type=jnp.float32
        )
        grad_tokens = jnp.einsum(
            "rne,de->rnd", grad_mix, out_weight, preferred_element_type=jnp.float32
        ).astype(jnp.bfloat16)
        grad_heads = lax.all_to_all(
            grad_tokens, "head", split_axis=2, concat_axis=1, tiled=True
        ).reshape(ROWS_MB, LOC, heads_here, DH)
        grad_query, key_grads, value_grads = attend_backward(
            grad_heads, queries, key_sets, value_sets, probability, weights, score_scale
        )
        remote_grads = [
            jnp.stack(
                [key_grads[1 + local_levels + bit_id], value_grads[1 + local_levels + bit_id]]
            ).reshape(2, ROWS_MB, BLOCK, part_width)
            for bit_id in range(seq_bits)
        ]
        level_grad = None
        for bit_id in reversed(range(seq_bits)):
            level_count = BLOCK * seq_count // 2**bit_id
            if level_grad is None:
                level_grad = jnp.zeros((2, ROWS_MB, level_count, part_width), jnp.float32)
            else:
                level_grad = spread_axis(level_grad, 2)
            group_id = seq_index // 2**bit_id
            sibling = group_id + 1 - 2 * (group_id % 2)
            held = lax.dynamic_slice_in_dim(level_grad, sibling * BLOCK, BLOCK, 2)
            level_grad = lax.dynamic_update_slice_in_dim(
                level_grad, held + remote_grads[bit_id], sibling * BLOCK, 2
            )
        summary_grad = sum_at_owner(level_grad.astype(jnp.bfloat16), "seq", 2)
        coarse_grad_key = summary_grad[0].reshape(ROWS_MB, BLOCK, heads_here, DH)
        coarse_grad_value = summary_grad[1].reshape(ROWS_MB, BLOCK, heads_here, DH)
        for level_id in reversed(range(local_levels)):
            coarse_grad_key = flip_blocks(key_grads[1 + level_id]) + spread_axis(coarse_grad_key, 1)
            coarse_grad_value = flip_blocks(value_grads[1 + level_id]) + spread_axis(
                coarse_grad_value, 1
            )
        grad_key = key_grads[0] + coarse_grad_key
        grad_value = value_grads[0] + coarse_grad_value
        grad_q = grad_query.astype(jnp.bfloat16).reshape(ROWS_MB, LOC, part_width)
        grad_k = grad_key.astype(jnp.bfloat16).reshape(ROWS_MB, LOC, part_width)
        grad_v = grad_value.astype(jnp.bfloat16).reshape(ROWS_MB, LOC, part_width)
        query_g = jnp.einsum("rnd,rne->de", normed, grad_q, preferred_element_type=jnp.float32)
        key_g = jnp.einsum("rnd,rne->de", normed, grad_k, preferred_element_type=jnp.float32)
        value_g = jnp.einsum("rnd,rne->de", normed, grad_v, preferred_element_type=jnp.float32)
        partial_sum = jnp.einsum(
            "rne,de->rnd", grad_q, query_part, preferred_element_type=jnp.float32
        )
        partial_sum = partial_sum + jnp.einsum(
            "rne,de->rnd", grad_k, key_part, preferred_element_type=jnp.float32
        )
        partial_sum = partial_sum + jnp.einsum(
            "rne,de->rnd", grad_v, value_part, preferred_element_type=jnp.float32
        )
        grad_normed = lax.psum_scatter(
            partial_sum.astype(jnp.bfloat16), "head", scatter_dimension=1, tiled=True
        ).astype(jnp.float32)
        unused_out, norm_one_back = jax.vjp(norm_rows, x_tokens, gain_first, shift_first)
        grad_input, gain_one_g, shift_one_g = norm_one_back(grad_normed)
        grad_rows.append((grad_residual + grad_input).astype(jnp.bfloat16))
        head_grads = (query_g, key_g, value_g)
        shared_raw = (
            out_g,
            up_g,
            down_g,
            up_bias_g,
            down_bias_g,
            gain_one_g,
            shift_one_g,
            gain_two_g,
            shift_two_g,
        )
        head_total = (
            head_grads if head_total is None else jax.tree.map(jnp.add, head_total, head_grads)
        )
        shared_total = (
            shared_raw if shared_total is None else jax.tree.map(jnp.add, shared_total, shared_raw)
        )
    head_total = lax.psum_scatter(head_total, "seq", scatter_dimension=0, tiled=True)
    shared_total = lax.psum_scatter(
        pack_shared(shared_total, seq_count, head_count),
        ("seq", "head"),
        scatter_dimension=0,
        tiled=True,
    )
    (
        out_sum,
        up_sum,
        down_sum,
        up_bias_sum,
        down_bias_sum,
        gain_one_sum,
        shift_one_sum,
        gain_two_sum,
        shift_two_sum,
    ) = shared_total
    return (
        jnp.concatenate(out_rows, axis=0),
        jnp.concatenate(grad_rows, axis=0),
        gain_one_sum,
        shift_one_sum,
        head_total[0],
        head_total[1],
        head_total[2],
        out_sum,
        gain_two_sum,
        shift_two_sum,
        up_sum,
        up_bias_sum,
        down_sum,
        down_bias_sum,
    )


def solution(mesh):
    placed = (
        P(None, ("seq", "head"), None),
        P(),
        P(),
        P(),
        P(),
        P(),
        P(),
        P(),
        P(),
        P(),
        P(),
        P(),
        P(),
        P(None, ("seq", "head"), None),
    )
    return jax.shard_map(
        body,
        mesh=mesh,
        in_specs=placed,
        out_specs=(
            P(None, ("seq", "head"), None),
            P(None, ("seq", "head"), None),
            P("seq"),
            P("seq"),
            P("seq", "head"),
            P("seq", "head"),
            P("seq", "head"),
            P("seq", "head"),
            P("seq"),
            P("seq"),
            P("seq", "head"),
            P("seq"),
            P("seq", "head"),
            P("seq"),
        ),
        check_vma=False,
    )
```

profile of v0, /device:TPU:0, one launch (start us, length us, event | category | flops | bytes accessed | tf_op | source)
XLA Modules:
  0.0 1584.6 jit_solution(14190780144849516322)
XLA Ops:
  9.9 15.6 all_gather.30
  28.4 14.4 all_gather.28
  60.3 9.3 all_gather.31
  78.6 9.3 all_gather.29
  105.0 4.6 all-to-all-start.2
  110.3 14.8 all_gather.24
  135.9 14.3 all_gather.26
  202.2 8.3 all_gather.25
  235.7 9.5 all_gather.27
  364.9 4.7 all-to-all-start.3
  371.6 3.8 all-to-all-done.3
  375.4 3.3 all-to-all-start.1
  380.4 4.0 all-to-all-done.1
  384.4 4.3 all-to-all-start
  391.6 2.6 all-to-all-done
  416.5 3.3 all-to-all-start.8
  425.5 3.9 all-to-all-start.10
  477.2 5.0 all-to-all-start.4
  535.6 5.3 all-to-all-start.6
  672.3 2.0 convolution_bitcast_fusion.17
  696.4 2.1 convolution_bitcast_fusion.16
  698.5 1.9 fusion.260
  718.7 2.2 convolution_bitcast_fusion.18
  720.9 2.0 fusion.264
  759.9 4.0 all-to-all-start.9
  879.6 1.9 fusion.266
  883.1 4.1 all-to-all-start.5
  892.8 4.2 all-to-all-start.11
  915.5 4.2 all-to-all-start.7
  961.6 1.9 fusion.39
  976.1 1.9 fusion.42
  985.2 20.3 %reduce-scatter.17.cloned.1.call-done = bf16[2,32,512]{2,1,0:T(8,128)(2,1)} async-done(((bf16[2,128,512]{2,1,0:T(8,128)(2,1)}), bf16[2,32,512]{2,1,0:T(8,128)(2,1)}) %reduce-scatter.17.cloned.1.call-update) | async-done | bytes 65552 | tf_op jit(solution)/shard_map/reduce_scatter | solution.py:330
  1005.5 20.1 %reduce-scatter.13.cloned.1.call-done = bf16[2,32,512]{2,1,0:T(8,128)(2,1)} async-done(((bf16[2,128,512]{2,1,0:T(8,128)(2,1)}), bf16[2,32,512]{2,1,0:T(8,128)(2,1)}) %reduce-scatter.13.cloned.1.call-update) | async-done | bytes 65552 | tf_op jit(solution)/shard_map/reduce_scatter | solution.py:330
  1031.0 2.3 fusion.73
  1033.4 2.1 convolution_bitcast_fusion.14
  1037.0 2.0 convolution_bitcast_fusion.12
  1044.4 2.2 fusion.76
  1056.4 4.1 bitcast_add_fusion
  1060.5 5.3 reshape.2841
  1065.8 4.8 copy.2555
  1074.3 2.9 bitcast_add_fusion.3
  1077.2 6.1 reshape.2838
  1083.3 5.5 copy.2554
  1089.4 3.1 fusion.117
  1099.1 52.1 %all-reduce.9.cloned.1.call-done = (f32[2048]{0:T(1024)}, f32[2048]{0:T(1024)}, f32[2048]{0:T(1024)}, f32[2048]{0:T(1024)}, f32[8192]{0:T(1024)}, /*index=5*/f32[2048]{0:T(1024)}) async-done(((f32[2048]{0:T(1024)}, f32[2048]{0:T(1024)}, f32[2048]{0:T(1024)}, f32[2048]{0:T(1024)}, f32[8192]{0:T(1024)}, /*index=5*/f32[2048]{0:T(1024)}), (f32[2048]{0:T(1024)}, f32[2048]{0:T(1024)}, f32[2048]{0:T(1024)}, ...) | async-done | bytes 73744
  1158.8 121.1 %reduce-scatter.25.cloned.1.call-done = f32[64,128]{1,0:T(8,128)} async-done(((f32[2048,128]{1,0:T(8,128)}), f32[64,128]{1,0:T(8,128)}) %reduce-scatter.25.cloned.1.call-update) | async-done | bytes 32784 | tf_op jit(solution)/shard_map/reduce_scatter | solution.py:355
  1279.8 147.9 %reduce-scatter.29.cloned.1.call-done = f32[256,128]{1,0:T(8,128)} async-done(((f32[8192,128]{1,0:T(8,128)}), f32[256,128]{1,0:T(8,128)}) %reduce-scatter.29.cloned.1.call-update) | async-done | bytes 131088 | tf_op jit(solution)/shard_map/reduce_scatter | solution.py:355
  1427.7 149.4 %reduce-scatter.27.cloned.1.call-done = f32[64,512]{1,0:T(8,128)} async-done(((f32[2048,512]{1,0:T(8,128)}), f32[64,512]{1,0:T(8,128)}) %reduce-scatter.27.cloned.1.call-update) | async-done | bytes 131088 | tf_op jit(solution)/shard_map/reduce_scatter | solution.py:355
  (1770 shorter events, 838.7 us)
Async XLA Ops:
  8.0 387.6 %copy-start = (bf16[512,2048]{1,0:T(8,128)(2,1)S(1)}, bf16[512,2048]{1,0:T(8,128)(2,1)}, u32[]{:S(2)}) copy-start(bf16[512,2048]{1,0:T(8,128)(2,1)} %param.23) | copy-start | bytes 6291460
  25.5 139.6 %copy-start.25 = (bf16[2,128,512]{2,1,0:T(8,128)(2,1)}, bf16[2,128,512]{2,1,0:T(8,128)(2,1)S(1)}, u32[]{:S(2)}) copy-start(bf16[2,128,512]{2,1,0:T(8,128)(2,1)S(1)} %all_gather.30) | copy-start | bytes 786436
  46.9 46.8 %copy-start.8 = (bf16[2,128,128]{1,2,0:T(8,128)(2,1)}, bf16[2,128,128]{1,2,0:T(8,128)(2,1)S(1)}, u32[]{:S(2)}) copy-start(bf16[2,128,128]{1,2,0:T(8,128)(2,1)S(1)} %convolution_convert_fusion.7) | copy-start | bytes 196612
  47.2 44.3 %copy-start.16 = (bf16[2,8,16,2,64]{4,3,2,1,0:T(2,128)(2,1)}, bf16[2,8,16,2,64]{4,3,2,1,0:T(2,128)(2,1)S(1)}, u32[]{:S(2)}) copy-start(bf16[2,8,16,2,64]{4,3,2,1,0:T(2,128)(2,1)S(1)} %reshape_reshape.172) | copy-start | bytes 196612
  47.3 28.1 %copy-start.48 = (bf16[2,4,32,2,64]{4,3,2,1,0:T(2,128)(2,1)}, bf16[2,4,32,2,64]{4,3,2,1,0:T(2,128)(2,1)S(1)}, u32[]{:S(2)}) copy-start(bf16[2,4,32,2,64]{4,3,2,1,0:T(2,128)(2,1)S(1)} %reshape_reshape.176) | copy-start | bytes 196612
  47.4 52.2 %copy-start.64 = (bf16[2,8,16,2,64]{4,3,2,1,0:T(2,128)(2,1)}, bf16[2,8,16,2,64]{4,3,2,1,0:T(2,128)(2,1)S(1)}, u32[]{:S(2)}) copy-start(bf16[2,8,16,2,64]{4,3,2,1,0:T(2,128)(2,1)S(1)} %reshape_reshape.170) | copy-start | bytes 196612
  47.7 43.7 %copy-start.61 = (bf16[2,8,16,2,64]{4,3,2,1,0:T(2,128)(2,1)}, bf16[2,8,16,2,64]{4,3,2,1,0:T(2,128)(2,1)S(1)}, u32[]{:S(2)}) copy-start(bf16[2,8,16,2,64]{4,3,2,1,0:T(2,128)(2,1)S(1)} %reshape_reshape.171) | copy-start | bytes 196612
  105.0 259.9 %all-to-all-start.2 = ((bf16[2,128,128]{2,0,1:T(2,128)(2,1)}), bf16[2,128,128]{2,0,1:T(2,128)(2,1)}, u32[]{:S(2)}, u32[]{:S(2)}) async-start(bf16[2,128,128]{2,0,1:T(2,128)(2,1)} %copy.2197), calls=%async_computation.2 | async-start | bytes 131072 | tf_op jit(solution)/shard_map/all_to_all | solution.py:242
  128.0 218.2 %copy-start.10 = (bf16[2,128,128]{1,2,0:T(8,128)(2,1)}, bf16[2,128,128]{1,2,0:T(8,128)(2,1)S(1)}, u32[]{:S(2)}) copy-start(bf16[2,128,128]{1,2,0:T(8,128)(2,1)S(1)} %convolution_convert_fusion.13) | copy-start | bytes 196612
  129.5 215.9 %copy-start.14 = (bf16[2,8,16,2,64]{4,3,2,1,0:T(2,128)(2,1)}, bf16[2,8,16,2,64]{4,3,2,1,0:T(2,128)(2,1)S(1)}, u32[]{:S(2)}) copy-start(bf16[2,8,16,2,64]{4,3,2,1,0:T(2,128)(2,1)S(1)} %reshape_reshape.146) | copy-start | bytes 196612
  153.1 170.6 %copy-start.6 = (bf16[2,128,128]{1,2,0:T(8,128)(2,1)}, bf16[2,128,128]{1,2,0:T(8,128)(2,1)S(1)}, u32[]{:S(2)}) copy-start(bf16[2,128,128]{1,2,0:T(8,128)(2,1)S(1)} %convolution_convert_fusion.10) | copy-start | bytes 196612
  155.9 164.2 %copy-start.18 = (bf16[2,8,16,2,64]{4,3,2,1,0:T(2,128)(2,1)}, bf16[2,8,16,2,64]{4,3,2,1,0:T(2,128)(2,1)S(1)}, u32[]{:S(2)}) copy-start(bf16[2,8,16,2,64]{4,3,2,1,0:T(2,128)(2,1)S(1)} %reshape_reshape.159) | copy-start | bytes 196612
  156.9 72.6 %copy-start.47 = (bf16[2,4,32,2,64]{4,3,2,1,0:T(2,128)(2,1)}, bf16[2,4,32,2,64]{4,3,2,1,0:T(2,128)(2,1)S(1)}, u32[]{:S(2)}) copy-start(bf16[2,4,32,2,64]{4,3,2,1,0:T(2,128)(2,1)S(1)} %reshape_reshape.163) | copy-start | bytes 196612
  166.3 124.7 %copy-start.12 = (bf16[2,128,128]{1,2,0:T(8,128)(2,1)}, bf16[2,128,128]{1,2,0:T(8,128)(2,1)S(1)}, u32[]{:S(2)}) copy-start(bf16[2,128,128]{1,2,0:T(8,128)(2,1)S(1)} %convolution_convert_fusion.4) | copy-start | bytes 196612
  166.6 118.3 %copy-start.20 = (bf16[2,8,16,2,64]{4,3,2,1,0:T(2,128)(2,1)}, bf16[2,8,16,2,64]{4,3,2,1,0:T(2,128)(2,1)S(1)}, u32[]{:S(2)}) copy-start(bf16[2,8,16,2,64]{4,3,2,1,0:T(2,128)(2,1)S(1)} %reshape_reshape.185) | copy-start | bytes 196612
  232.3 33.1 %copy-start.49 = (bf16[2,4,32,2,64]{4,3,2,1,0:T(2,128)(2,1)S(1)}, bf16[2,4,32,2,64]{4,3,2,1,0:T(2,128)(2,1)}, u32[]{:S(2)}) copy-start(bf16[2,4,32,2,64]{4,3,2,1,0:T(2,128)(2,1)} %reshape_reshape.189) | copy-start | bytes 196612
  235.7 103.2 %copy-start.143 = (bf16[2,2,2,16,2,64]{5,3,2,1,4,0:T(8,128)(2,1)}, bf16[2,2,2,16,2,64]{5,3,2,1,4,0:T(8,128)(2,1)S(1)}, u32[]{:S(2)}) copy-start(bf16[2,2,2,16,2,64]{5,3,2,1,4,0:T(8,128)(2,1)S(1)} %rev.146) | copy-start | bytes 98308
  248.6 75.1 %copy-start.205 = (bf16[2,16,2,64]{3,2,1,0:T(2,128)(2,1)}, bf16[2,16,2,64]{3,2,1,0:T(2,128)(2,1)S(1)}, u32[]{:S(2)}) copy-start(bf16[2,16,2,64]{3,2,1,0:T(2,128)(2,1)S(1)} %reshape.2628) | copy-start | bytes 24580
  256.8 28.2 %copy-start.45 = (bf16[2,2,64,2,64]{4,2,3,1,0:T(8,128)(2,1)}, bf16[2,2,64,2,64]{4,2,3,1,0:T(8,128)(2,1)S(1)}, u32[]{:S(2)}) copy-start(bf16[2,2,64,2,64]{4,2,3,1,0:T(8,128)(2,1)S(1)} %copy.2214) | copy-start | bytes 196612
  364.9 10.5 all-to-all-start.3
  375.4 9.0 all-to-all-start.1
  384.4 9.7 all-to-all-start
  416.5 9.0 all-to-all-start.8
  425.5 51.7 %all-to-all-start.10 = ((bf16[4,2,4096]{2,1,0:T(2,128)(2,1)}), bf16[4,2,4096]{2,1,0:T(2,128)(2,1)}, u32[]{:S(2)}, u32[]{:S(2)}) async-start(bf16[4,2,4096]{2,1,0:T(2,128)(2,1)} %reshape.2914), calls=%async_computation.13 | async-start | bytes 131072 | tf_op jit(solution)/shard_map/all_to_all | solution.py:280
  477.2 58.4 %all-to-all-start.4 = ((bf16[4,2,4096]{2,1,0:T(2,128)(2,1)}), bf16[4,2,4096]{2,1,0:T(2,128)(2,1)}, u32[]{:S(2)}, u32[]{:S(2)}) async-start(bf16[4,2,4096]{2,1,0:T(2,128)(2,1)} %reshape.2918), calls=%async_computation.4 | async-start | bytes 131072 | tf_op jit(solution)/shard_map/all_to_all | solution.py:280
  535.6 58.7 %all-to-all-start.6 = ((bf16[4,2,4096]{2,1,0:T(2,128)(2,1)}), bf16[4,2,4096]{2,1,0:T(2,128)(2,1)}, u32[]{:S(2)}, u32[]{:S(2)}) async-start(bf16[4,2,4096]{2,1,0:T(2,128)(2,1)} %reshape.2920), calls=%async_computation.7 | async-start | bytes 131072 | tf_op jit(solution)/shard_map/all_to_all | solution.py:280
  759.9 123.2 %all-to-all-start.9 = ((bf16[8,2,2,16,128]{4,3,2,1,0:T(8,128)(2,1)}), bf16[8,2,2,16,128]{4,3,2,1,0:T(8,128)(2,1)}, u32[]{:S(2)}, u32[]{:S(2)}) async-start(bf16[8,2,2,16,128]{4,3,2,1,0:T(8,128)(2,1)} %bitcast.1568), calls=%async_computation.11 | async-start | bytes 262144 | tf_op jit(solution)/shard_map/all_to_all | solution.py:24
  883.1 9.7 all-to-all-start.5
  892.8 22.6 %all-to-all-start.11 = ((bf16[8,2,2,16,128]{4,3,2,1,0:T(8,128)(2,1)}), bf16[8,2,2,16,128]{4,3,2,1,0:T(8,128)(2,1)}, u32[]{:S(2)}, u32[]{:S(2)}) async-start(bf16[8,2,2,16,128]{4,3,2,1,0:T(8,128)(2,1)} %bitcast.1745), calls=%async_computation.14 | async-start | bytes 262144 | tf_op jit(solution)/shard_map/all_to_all | solution.py:24
  915.5 15.5 all-to-all-start.7
  919.6 64.4 %reduce-scatter.15.cloned.1.call-start = ((), (), s32[]{:S(2)}) async-start(), calls=%async_computation.24 | async-start | bytes 327680 | tf_op jit(solution)/shard_map/reduce_scatter | solution.py:330
  940.7 44.5 %reduce-scatter.11.cloned.1.call-start = ((), (), s32[]{:S(2)}) async-start(), calls=%async_computation.22 | async-start | bytes 327680 | tf_op jit(solution)/shard_map/reduce_scatter | solution.py:330
  963.5 41.9 %reduce-scatter.17.cloned.1.call-start = ((), (), s32[]{:S(2)}) async-start(), calls=%async_computation.25 | async-start | bytes 327680 | tf_op jit(solution)/shard_map/reduce_scatter | solution.py:330
  978.1 47.5 %reduce-scatter.13.cloned.1.call-start = ((), (), s32[]{:S(2)}) async-start(), calls=%async_computation.23 | async-start | bytes 327680 | tf_op jit(solution)/shard_map/reduce_scatter | solution.py:330
  980.9 50.1 %copy-start.278 = (f32[2,128]{1,0:T(2,128)S(1)}, f32[2,128]{1,0:T(2,128)}, u32[]{:S(2)}) copy-start(f32[2,128]{1,0:T(2,128)} %copy-done.277) | copy-start | bytes 3076
  983.9 167.3 %all-reduce.9.cloned.1.call-start = ((), (), s32[]{:S(2)}) async-start(), calls=%async_computation.32 | async-start | bytes 147456
  985.0 44.4 %copy-start.283 = (f32[2,32]{1,0:T(2,128)}, f32[2,32]{1,0:T(2,128)S(1)}, u32[]{:S(2)}) copy-start(f32[2,32]{1,0:T(2,128)S(1)} %broadcast_multiply_fusion.11) | copy-start | bytes 772
  985.1 44.4 %copy-start.285 = (f32[2,32]{1,0:T(2,128)}, f32[2,32]{1,0:T(2,128)S(1)}, u32[]{:S(2)}) copy-start(f32[2,32]{1,0:T(2,128)S(1)} %broadcast_multiply_fusion.10) | copy-start | bytes 772
  985.1 44.4 %copy-start.287 = (f32[2,32]{1,0:T(2,128)}, f32[2,32]{1,0:T(2,128)S(1)}, u32[]{:S(2)}) copy-start(f32[2,32]{1,0:T(2,128)S(1)} %broadcast_multiply_fusion.8) | copy-start | bytes 772
  985.1 42.3 %copy-start.292 = (f32[2,32]{1,0:T(2,128)}, f32[2,32]{1,0:T(2,128)S(1)}, u32[]{:S(2)}) copy-start(f32[2,32]{1,0:T(2,128)S(1)} %get-tuple-element.176) | copy-start | bytes 772
  985.1 44.3 %copy-start.290 = (f32[2,32]{1,0:T(2,128)}, f32[2,32]{1,0:T(2,128)S(1)}, u32[]{:S(2)}) copy-start(f32[2,32]{1,0:T(2,128)S(1)} %get-tuple-element.175) | copy-start | bytes 772
  1031.0 127.8 %reduce-scatter.19.cloned.1.call-start = ((), (), s32[]{:S(2)}) async-start(), calls=%async_computation.26 | async-start | bytes 294912 | tf_op jit(solution)/shard_map/reduce_scatter | solution.py:354
  1033.4 125.4 %reduce-scatter.23.cloned.1.call-start = ((), (), s32[]{:S(2)}) async-start(), calls=%async_computation.28 | async-start | bytes 294912 | tf_op jit(solution)/shard_map/reduce_scatter | solution.py:354
  1043.1 115.7 %reduce-scatter.21.cloned.1.call-start = ((), (), s32[]{:S(2)}) async-start(), calls=%async_computation.27 | async-start | bytes 294912 | tf_op jit(solution)/shard_map/reduce_scatter | solution.py:354
  1046.6 233.2 %reduce-scatter.25.cloned.1.call-start = ((), (), s32[]{:S(2)}) async-start(), calls=%async_computation.29 | async-start | bytes 1081344 | tf_op jit(solution)/shard_map/reduce_scatter | solution.py:355
  1051.2 376.5 %reduce-scatter.29.cloned.1.call-start = ((), (), s32[]{:S(2)}) async-start(), calls=%async_computation.31 | async-start | bytes 4325376 | tf_op jit(solution)/shard_map/reduce_scatter | solution.py:355
  1070.7 506.4 %reduce-scatter.27.cloned.1.call-start = ((), (), s32[]{:S(2)}) async-start(), calls=%async_computation.30 | async-start | bytes 4325376 | tf_op jit(solution)/shard_map/reduce_scatter | solution.py:355
  1095.6 481.5 %copy-start.1 = (bf16[512,2048]{1,0:T(8,128)(2,1)S(1)}, bf16[512,2048]{1,0:T(8,128)(2,1)}, u32[]{:S(2)}) copy-start(bf16[512,2048]{1,0:T(8,128)(2,1)} %param.23) | copy-start | bytes 6291460
  (329 other events, 2528.1 us)
Sparse Core Ops, SparseCore 0:
  940.8 21.5 reduce-scatter.14
  965.3 19.8 reduce-scatter.10
  987.4 18.0 reduce-scatter.16
  1007.7 17.7 reduce-scatter.12
  1031.8 119.3 all-reduce.8
Sparse Core Ops, SparseCore 1:
  1035.0 32.0 reduce-scatter.18
  1070.8 33.7 reduce-scatter.22
  1108.0 33.6 reduce-scatter.20
  1144.6 135.2 reduce-scatter.24
  1282.7 144.9 reduce-scatter.28
  1430.6 146.4 reduce-scatter.26
where the time goes:
time: 1610 us; the launch traced here: 1580 us
  waiting for transfers between devices  524 us (33%)
  local copies, waits for them, and re-layouts  514 us (32%)
  matrix products  274 us (17%)
  other arithmetic  103 us (6%)
  blocking collectives  95.6 us (6%)
  starting transfers between devices  51.8 us (3%)
  between operations  22.1 us (1%)
    reduce_scatter x3, waiting for transfers between devices, body(): lax.psum_scatter(pack_shared(shared_total, seq_count, head_count), ('seq'...  418 us
    dot_general x56, matrix products, group_keys(): jnp.einsum('rbmhk,rbmhd->rbkhd', weight_view, left_view, preferred_elemen...  75.6 us
    dot_general x56, matrix products, group_values(): jnp.einsum('rbmhk,rbkhd->rbmhd', left_view, right_view, preferred_element...  60.6 us
    all_gather x4, blocking collectives, body(): x_gathered = lax.all_gather(x_local, 'head', axis=1, tiled=True)  59.2 us
    reshape x40, local copies, waits for them, and re-layouts, group_values(): product.reshape(shape_in[0], shape_in[1], shape_in[2], right.shape[3])  58.1 us
    unnamed x12, waiting for transfers between devices  52.3 us
    rev x44, local copies, waits for them, and re-layouts, flip_blocks(): return split_view[:, :, ::-1].reshape(shape_in)  45.6 us
    unnamed x756, local copies, waits for them, and re-layouts  43.2 us
  transfers between devices with their start and end apart: 23, of which 11 were waited for; matrix products, arithmetic and copies ran while one was open for 40% of the time, Pallas kernels for 0%

commit v1 on v0

v1 whole, which is shorter than its diff:
```python
import functools

import jax
import jax.numpy as jnp
from jax import lax
from jax.experimental import pallas as pl
from jax.experimental.pallas import tpu as pltpu
from jax.sharding import PartitionSpec as P

MESH = pl.DeviceIdType.MESH
BF = jnp.bfloat16
F32 = jnp.float32
DH = 64
BLOCK = 16
EPSILON = 1e-05
PAIR = 2 * DH
VEC_ROWS = 16


def idiv(value, k):
    return lax.div(value, jnp.int32(k))


def irem(value, k):
    return lax.rem(value, jnp.int32(k))


def bit_of(value, b):
    return irem(idiv(value, 1 << b), 2)


def flip(value, k):
    b = 0
    while k >> b:
        if (k >> b) & 1:
            value = value + (1 - 2 * bit_of(value, b)) * (1 << b)
        b += 1
    return value


def dot(a, b):
    return jnp.dot(a, b, preferred_element_type=F32)


def dot_t(a, b):
    return lax.dot_general(a, b, (((1,), (1,)), ((), ())), preferred_element_type=F32)


def t_dot(a, b):
    return lax.dot_general(a, b, (((0,), (0,)), ((), ())), preferred_element_type=F32)


def two_part_dot(a, b):
    high = b.astype(BF)
    low = (b - high.astype(F32)).astype(BF)
    return dot(a, high) + dot(a, low)


def pair_mean(rows):
    i = lax.broadcasted_iota(jnp.int32, (rows // 2, rows), 0)
    j = lax.broadcasted_iota(jnp.int32, (rows // 2, rows), 1)
    return jnp.where((j >> 1) == i, 0.5, 0.0).astype(BF)


class Plan:
    def __init__(self, seq, head, rows, pos, width, hidden):
        self.seq, self.head, self.rows, self.pos, self.width, self.hidden = seq, head, rows, pos, width, hidden
        self.minor = rows // head
        self.groups = seq // self.minor
        self.tokens = rows * pos
        self.pairs = width // PAIR
        self.local = (self.tokens // BLOCK).bit_length() - 1
        self.remote = self.groups.bit_length() - 1
        self.bits = seq.bit_length() - 1
        self.far = self.tokens * 2 - 2 * BLOCK
        keys = self.far + BLOCK * max(self.remote, 2)
        self.keys = -(-keys // 128) * 128
        self.blocks = {
            "down": (hidden // seq, width // head),
            "up": (width // seq, hidden // head),
            "out": (width // seq, width // head),
            "query": (width // seq, width // head),
            "key": (width // seq, width // head),
            "value": (width // seq, width // head),
        }
        straight = list(range(self.bits))
        turned = straight[:1] + straight[:0:-1]
        self.order = {
            "down": straight,
            "up": turned,
            "out": straight,
            "query": turned,
            "key": straight,
            "value": turned,
        }


class Summed:
    def __init__(self, plan, me, name, number, grad, got, got_head, send, recv, out):
        self.plan, self.name, self.number = plan, name, number
        self.s, self.h = me
        self.grad, self.got, self.got_head, self.out = grad, got, got_head, out
        self.send, self.recv = send, recv
        self.order = plan.order[name]
        self.started = []

    def index(self, fixed, other=None):
        at = []
        for b in reversed(range(self.plan.bits)):
            if b == other:
                at.append(1 - bit_of(self.s, b))
            elif b in fixed:
                at.append(bit_of(self.s, b))
            else:
                at.append(slice(None))
        return tuple(at)

    def put(self, s, h, value):
        at = tuple((s >> b) & 1 for b in reversed(range(self.plan.bits)))
        self.grad[at + (h,)] = value.astype(BF)

    def start(self, stage):
        b = self.order[stage]
        copy = pltpu.make_async_remote_copy(
            src_ref=self.grad.at[self.index(self.order[:stage], b)],
            dst_ref=self.got[stage],
            send_sem=self.send.at[self.number, stage],
            recv_sem=self.recv.at[self.number, stage],
            device_id=(flip(self.s, 1 << b), self.h),
            device_id_type=MESH,
        )
        copy.start()
        self.started.append(copy)

    def finish(self, stage):
        self.started[stage].wait_recv()
        at = self.index(self.order[: stage + 1])
        free = [n for n, a in zip(self.grad.shape, at) if isinstance(a, slice)] + [self.plan.head]
        combos = [()]
        for n in free:
            combos = [c + (i,) for c in combos for i in range(n)]
        for combo in combos:
            left = list(combo)
            full = tuple(left.pop(0) if isinstance(a, slice) else a for a in at) + (left.pop(0),)
            self.grad[full] = self.grad[full] + self.got[stage][combo]

    def start_head(self):
        at = self.index(self.order)
        for k in range(1, self.plan.head):
            peer = flip(self.h, k)
            copy = pltpu.make_async_remote_copy(
                src_ref=self.grad.at[at + (peer,)],
                dst_ref=self.got_head.at[k - 1],
                send_sem=self.send.at[self.number, self.plan.bits + k - 1],
                recv_sem=self.recv.at[self.number, self.plan.bits + k - 1],
                device_id=(self.s, peer),
                device_id_type=MESH,
            )
            copy.start()
            self.started.append(copy)

    def finish_head(self):
        total = self.grad[self.index(self.order) + (self.h,)].astype(F32)
        for k in range(1, self.plan.head):
            self.started[self.plan.bits + k - 1].wait_recv()
            total = total + self.got_head[k - 1].astype(F32)
        self.out[...] = total

    def drain(self):
        for copy in self.started:
            copy.wait_send()


def layer_kernel(plan, *refs):
    refs = list(refs)

    def take(n):
        taken = refs[:n]
        del refs[:n]
        return taken

    x_in, dy_in, gain_one, shift_one, gain_two, shift_two, up_bias, down_bias = take(8)
    weights_in = take(6)
    lo_out, ig_out = take(2)
    grads_out = take(6)
    (vec_out,) = take(1)
    xg, dyg, log, igg = take(4)
    wq, wk, wv, wo, wu, wd = weights = take(6)
    norm_b, n_one, rs_one, n_two, rs_two, norm_two_b, residual, d_residual = take(8)
    q_ref, k_ref, v_ref, prob_ref, mask_ref, mixed_ref = take(6)
    act_ref, slope_ref, dh_ref = take(3)
    dmixed_ref, dq_ref, dk_ref, dv_ref, far_ref = take(5)
    c_send, c_got, d_send, d_got = take(4)
    names = list(plan.blocks)
    grads = take(6)
    gots = [take(plan.bits) for _ in names]
    got_heads = take(6)
    vec_bufs, vec_got = take(2)
    send_a, recv_a, send_r, recv_r, send_s, recv_s, here = take(7)
    assert not refs

    seq, head, rows, width, tokens = plan.seq, plan.head, plan.rows, plan.width, plan.tokens
    s, h = lax.axis_index("seq"), lax.axis_index("head")
    c, g = irem(s, plan.minor), idiv(s, plan.minor)
    j = c * head + h

    def group_peer(k):
        other = flip(j, k)
        return other, (g * plan.minor + idiv(other, head), irem(other, head))

    def row_peer(k):
        other = flip(g, k)
        return other, (other * plan.minor + c, h)

    barrier = pltpu.get_barrier_semaphore()
    peers = {}
    for k in range(1, rows):
        peers[("group", k)] = group_peer(k)[1]
    for k in range(1, plan.groups):
        peers[("row", k)] = row_peer(k)[1]
    for device in peers.values():
        pl.semaphore_signal(barrier, inc=1, device_id=device, device_id_type=MESH)

    loads = [pltpu.make_async_copy(a, b, here.at[i]) for i, (a, b) in enumerate(zip(weights_in, weights))]
    for i in (1, 2, 0, 3, 4, 5):
        loads[i].start()
    own = [
        pltpu.make_async_copy(x_in.at[j], xg.at[j], here.at[6]),
        pltpu.make_async_copy(dy_in.at[j], dyg.at[j], here.at[7]),
    ]
    for copy in own:
        copy.start()

    i_q = lax.broadcasted_iota(jnp.int32, (tokens, plan.keys), 0)
    i_k = lax.broadcasted_iota(jnp.int32, (tokens, plan.keys), 1)
    valid = (i_k < tokens) & ((i_q >> 5) == (i_k >> 5))
    first = tokens
    for level in range(1, plan.local):
        count = tokens >> level
        block = (i_k - first) >> 4
        here_level = (i_k >= first) & (i_k < first + count)
        valid = valid | (here_level & (((i_q >> (4 + level)) ^ 1) == block))
        first += count
    valid = valid | ((i_k >= plan.far) & (i_k < plan.far + BLOCK * plan.remote))
    mask_ref[...] = jnp.where(valid, 0.0, -1e30).astype(F32)

    pl.semaphore_wait(barrier, len(peers))

    def exchange(number, source, target):
        copies = []
        for k in range(1, rows):
            other, device = group_peer(k)
            copy = pltpu.make_async_remote_copy(
                src_ref=source.at[other],
                dst_ref=target.at[j],
                send_sem=send_a.at[number, k],
                recv_sem=recv_a.at[number, k],
                device_id=device,
                device_id_type=MESH,
            )
            copy.start()
            copies.append(copy)
        return copies

    x_copies = exchange(0, x_in, xg)
    dy_copies = exchange(1, dy_in, dyg)

    def norm_stats(values):
        center = values - jnp.mean(values, axis=-1, keepdims=True)
        spread = jnp.mean(center * center, axis=-1, keepdims=True)
        scale = lax.rsqrt(spread + EPSILON)
        return center * scale, scale

    def norm_back(d_norm, n, scale, gain):
        weighted = d_norm * gain
        return scale * (
            weighted
            - jnp.mean(weighted, axis=-1, keepdims=True)
            - n * jnp.mean(weighted * n, axis=-1, keepdims=True)
        )

    def store_pairs(ref, first, value):
        for p in range(plan.pairs):
            ref[p, first : first + value.shape[0], :] = value[:, p * PAIR : (p + 1) * PAIR]

    own[0].wait()
    for copy in x_copies:
        copy.wait_recv()
    x = xg[...].reshape(tokens, width).astype(F32)
    n, scale = norm_stats(x)
    n_one[...] = n
    rs_one[...] = scale
    normed = (n * gain_one[...] + shift_one[...]).astype(BF)
    norm_b[...] = normed
    for index, (w, load, ref) in enumerate(((wk, loads[1], k_ref), (wv, loads[2], v_ref))):
        load.wait()
        level = dot(normed, w[...]).astype(BF)
        store_pairs(ref, 0, level)
        first = tokens
        for l in range(plan.local):
            level = dot(pair_mean(level.shape[0]), level).astype(BF)
            if l + 1 < plan.local:
                store_pairs(ref, first, level)
                first += level.shape[0]
        c_send[index] = level
    c_copies = []
    for k in range(1, plan.groups):
        other, device = row_peer(k)
        copy = pltpu.make_async_remote_copy(
            src_ref=c_send,
            dst_ref=c_got.at[g],
            send_sem=send_r.at[0, k],
            recv_sem=recv_r.at[0, k],
            device_id=device,
            device_id_type=MESH,
        )
        copy.start()
        c_copies.append(copy)
    loads[0].wait()
    store_pairs(q_ref, 0, (dot(normed, wq[...]) * (DH**-0.5)).astype(BF))

    for copy in c_copies:
        copy.wait_recv()
    for index, ref in enumerate((k_ref, v_ref)):
        for b in range(plan.remote):
            upper = idiv(g, 1 << b)
            base = (upper + 1 - 2 * irem(upper, 2)) * (1 << b)
            level = c_got[pl.ds(base, 1 << b), index].reshape(BLOCK << b, width)
            for _ in range(b):
                level = dot(pair_mean(level.shape[0]), level).astype(BF)
            store_pairs(ref, plan.far + BLOCK * b, level)
        end = plan.far + BLOCK * plan.remote
        if end < plan.keys:
            store_pairs(ref, end, jnp.zeros((plan.keys - end, width), BF))

    lane = lax.broadcasted_iota(jnp.int32, (1, PAIR), 1)
    low = lane < DH

    def only(e, value):
        return jnp.where(low if e == 0 else ~low, value, jnp.zeros_like(value))

    def attend(p, carry):
        q, k, v = q_ref[p], k_ref[p], v_ref[p]
        mixed = []
        for e in range(2):
            scores = dot_t(only(e, q), k) + mask_ref[...]
            top = jnp.max(scores, axis=-1, keepdims=True)
            raised = jnp.exp(scores - top)
            prob = raised / jnp.sum(raised, axis=-1, keepdims=True)
            prob_ref[2 * p + e] = prob
            mixed.append(dot(prob.astype(BF), v))
        mixed_ref[p] = jnp.where(low, mixed[0], mixed[1]).astype(BF)
        return carry

    lax.fori_loop(0, plan.pairs, attend, 0)

    def joined(ref):
        return jnp.concatenate([ref[p] for p in range(plan.pairs)], axis=1)

    loads[3].wait()
    mixed = joined(mixed_ref)
    res = xg[...].reshape(tokens, width).astype(F32) + dot(mixed, wo[...])
    residual[...] = res
    n, scale = norm_stats(res)
    n_two[...] = n
    rs_two[...] = scale
    norm_two_b[...] = (n * gain_two[...] + shift_two[...]).astype(BF)

    sums = [
        Summed(plan, (s, h), name, i, grads[i], gots[i], got_heads[i], send_s, recv_s, grads_out[i])
        for i, name in enumerate(names)
    ]
    down, up, out, query, key, value = sums
    row = lambda a: jnp.sum(a, axis=0, keepdims=True)

    def put_all(target, block, first_row, first_col):
        r, w = plan.blocks[target.name]
        for a in range(0, block.shape[0], r):
            for b in range(0, block.shape[1], w):
                target.put((first_row + a) // r, (first_col + b) // w, block[a : a + r, b : b + w])

    loads[4].wait()
    loads[5].wait()
    own[1].wait()
    for copy in dy_copies:
        copy.wait_recv()
    chunk = 512
    dy = dyg[...].reshape(tokens, width)
    for f in range(0, plan.hidden, chunk):
        hid = dot(norm_two_b[...], wu[:, f : f + chunk]) + up_bias[:, f : f + chunk]
        cdf = 0.5 * (1.0 + lax.erf(hid * (0.5**0.5)))
        act = (hid * cdf).astype(BF)
        act_ref[:, f : f + chunk] = act
        slope_ref[:, f : f + chunk] = cdf + hid * (jnp.exp(-0.5 * hid * hid) * 0.3989422804014327)
        put_all(down, t_dot(act, dy), f, 0)
    down.start(0)

    hidden_rows = []
    for f in range(0, plan.hidden, chunk):
        dh = (dot_t(dy, wd[f : f + chunk, :]) * slope_ref[:, f : f + chunk]).astype(BF)
        dh_ref[:, f : f + chunk] = dh
        hidden_rows.append(row(dh.astype(F32)))
        put_all(up, t_dot(norm_two_b[...], dh), 0, f)
    up.start(0)
    down.finish(0)
    down.start(1)

    d_norm_two = dot_t(dh_ref[...], wu[...])
    n = n_two[...]
    dy_f = dy.astype(F32)
    vec_bufs[0, 2:3, :] = row(d_norm_two * n)
    vec_bufs[0, 3:4, :] = row(d_norm_two)
    vec_bufs[0, 4:5, :] = row(dy_f)
    per = plan.hidden // width
    for i in range(per):
        flat = jnp.concatenate(hidden_rows, axis=1)
        vec_bufs[0, 5 + i : 6 + i, :] = flat[:, i * width : (i + 1) * width]
    d_res = dy_f + norm_back(d_norm_two, n, rs_two[...], gain_two[...])
    d_residual[...] = d_res
    d_mix = d_res.astype(BF)
    put_all(out, t_dot(joined(mixed_ref), d_mix), 0, 0)
    out.start(0)
    store_pairs(dmixed_ref, 0, dot_t(d_mix, wo[...]).astype(BF))
    up.finish(0)
    up.start(1)

    result = residual[...] + dot(act_ref[...], wd[...]) + down_bias[...]
    log[...] = result.astype(BF).reshape(rows, plan.pos, width)
    lo_copies = exchange(2, log, lo_out)
    lo_own = pltpu.make_async_copy(log.at[j], lo_out.at[j], here.at[8])
    lo_own.start()
    out.finish(0)
    out.start(1)

    i_t = lax.broadcasted_iota(jnp.int32, (tokens, tokens), 0)
    i_c = lax.broadcasted_iota(jnp.int32, (tokens, tokens), 1)
    spread = jnp.zeros((tokens, tokens), F32)
    first = 0
    for level in range(1, plan.local):
        count = tokens >> level
        spread = spread + jnp.where((i_t >> level) == (i_c - first), 0.5**level, 0.0)
        first += count
    spread = spread.astype(BF)

    def attend_back(p, carry):
        q, k, v, dm = q_ref[p], k_ref[p], v_ref[p], dmixed_ref[p]
        dq, dk, dv = [], 0.0, 0.0
        for e in range(2):
            dm_e = only(e, dm)
            prob = prob_ref[2 * p + e]
            d_prob = dot_t(dm_e, v)
            inner = jnp.sum(prob * d_prob, axis=-1, keepdims=True)
            d_scores = (prob * (d_prob - inner)).astype(BF)
            dq.append(dot(d_scores, k))
            dk = dk + t_dot(d_scores, only(e, q))
            dv = dv + t_dot(prob.astype(BF), dm_e)
        dq_ref[p] = (jnp.where(low, dq[0], dq[1]) * (DH**-0.5)).astype(BF)
        for index, (total, ref) in enumerate(((dk, dk_ref), (dv, dv_ref))):
            ref[p] = total[:tokens] + two_part_dot(spread, total[tokens : 2 * tokens])
            far_ref[index, p] = total[plan.far :]
        return carry

    half = plan.pairs // 2
    lax.fori_loop(0, half, attend_back, 0)
    down.finish(1)
    down.start(2)
    lax.fori_loop(half, plan.pairs, attend_back, 0)

    i_a = lax.broadcasted_iota(jnp.int32, (BLOCK, BLOCK), 0)
    i_b = lax.broadcasted_iota(jnp.int32, (BLOCK, BLOCK), 1)
    d_copies = []
    for k in range(1, plan.groups):
        other, device = row_peer(k)
        b = k.bit_length() - 1
        offset = irem(other, 1 << b)
        pick = jnp.where(((offset * BLOCK + i_a) >> b) == i_b, 0.5**b, 0.0).astype(BF)
        for index in range(2):
            for p in range(plan.pairs):
                level = far_ref[index, p, BLOCK * b : BLOCK * (b + 1), :].astype(BF)
                d_send[k, index, p] = dot(pick, level).astype(BF)
        copy = pltpu.make_async_remote_copy(
            src_ref=d_send.at[k],
            dst_ref=d_got.at[k],
            send_sem=send_r.at[1, k],
            recv_sem=recv_r.at[1, k],
            device_id=device,
            device_id_type=MESH,
        )
        copy.start()
        d_copies.append(copy)

    normed = norm_b[...]
    d_query = joined(dq_ref)
    put_all(query, t_dot(normed, d_query), 0, 0)
    query.start(0)
    up.finish(1)
    up.start(2)
    d_normed = dot_t(d_query, wq[...])
    out.finish(1)
    out.start(2)

    for copy in d_copies:
        copy.wait_recv()
    i_t = lax.broadcasted_iota(jnp.int32, (tokens, BLOCK), 0)
    i_c = lax.broadcasted_iota(jnp.int32, (tokens, BLOCK), 1)
    last = jnp.where((i_t >> plan.local) == i_c, 0.5**plan.local, 0.0).astype(BF)
    for index, (ref, w, target) in enumerate(((dk_ref, wk, key), (dv_ref, wv, value))):
        pieces = []
        for p in range(plan.pairs):
            total = ref[p]
            if plan.groups > 1:
                coarse = d_got[1, index, p].astype(F32)
                for k in range(2, plan.groups):
                    coarse = coarse + d_got[k, index, p].astype(F32)
                total = total + two_part_dot(last, coarse)
            pieces.append(total.astype(BF))
        d_part = jnp.concatenate(pieces, axis=1)
        put_all(target, t_dot(normed, d_part), 0, 0)
        target.start(0)
        d_normed = d_normed + dot_t(d_part, w[...])
    query.finish(0)
    query.start(1)

    n = n_one[...]
    vec_bufs[0, 0:1, :] = row(d_normed * n)
    vec_bufs[0, 1:2, :] = row(d_normed)
    for i in range(5 + per, VEC_ROWS):
        vec_bufs[0, i : i + 1, :] = jnp.zeros((1, width), F32)

    vec_copies = []

    def vec_start(stage):
        if stage < plan.bits:
            jobs = [(stage, (flip(s, 1 << stage), h))]
        else:
            jobs = [(plan.bits + k - 1, (s, flip(h, k))) for k in range(1, head)]
        for slot, device in jobs:
            copy = pltpu.make_async_remote_copy(
                src_ref=vec_bufs.at[min(slot, plan.bits)],
                dst_ref=vec_got.at[slot],
                send_sem=send_s.at[6, slot],
                recv_sem=recv_s.at[6, slot],
                device_id=device,
                device_id_type=MESH,
            )
            copy.start()
            vec_copies.append(copy)

    def vec_finish(stage):
        vec_copies[stage].wait_recv()
        vec_bufs[stage + 1] = vec_bufs[stage] + vec_got[stage]

    vec_start(0)
    d_first = norm_back(d_normed, n, rs_one[...], gain_one[...])
    igg[...] = (d_residual[...] + d_first).astype(BF).reshape(rows, plan.pos, width)
    ig_copies = exchange(3, igg, ig_out)
    ig_own = pltpu.make_async_copy(igg.at[j], ig_out.at[j], here.at[9])
    ig_own.start()

    key.finish(0)
    key.start(1)
    value.finish(0)
    value.start(1)
    vec_finish(0)
    done = {"down": 2, "up": 2, "out": 2, "query": 1, "key": 1, "value": 1}
    vec_done = 1
    while True:
        if vec_done <= plan.bits:
            vec_start(vec_done)
        for item in sums:
            stage = done[item.name]
            if stage < plan.bits:
                item.finish(stage)
                if stage + 1 < plan.bits:
                    item.start(stage + 1)
                else:
                    item.start_head()
            done[item.name] = stage + 1
        if vec_done < plan.bits:
            vec_finish(vec_done)
        vec_done += 1
        if vec_done > plan.bits and all(stage >= plan.bits for stage in done.values()):
            break
    for item in sums:
        item.finish_head()
    near = vec_bufs[plan.bits]
    parts = []
    for k in range(1, head):
        vec_copies[plan.bits + k - 1].wait_recv()
        parts.append(vec_got[plan.bits + k - 1])
    values = [near] + parts
    while len(values) > 1:
        values = [values[i] + values[i + 1] for i in range(0, len(values), 2)]
    vec_out[...] = values[0]

    for copy in lo_copies + ig_copies:
        copy.wait_recv()
    lo_own.wait()
    ig_own.wait()
    for copy in x_copies + dy_copies + lo_copies + ig_copies + c_copies + d_copies + vec_copies:
        copy.wait_send()
    for item in sums:
        item.drain()


def body(
    inputs,
    gain_first,
    shift_first,
    query_weight,
    key_weight,
    value_weight,
    out_weight,
    gain_second,
    shift_second,
    up_weight,
    up_bias,
    down_weight,
    down_bias,
    cotangent,
):
    rows, pos, width = inputs.shape
    hidden = up_weight.shape[1]
    plan = Plan(lax.axis_size("seq"), lax.axis_size("head"), rows, pos, width, hidden)
    tokens, keys, pairs, groups, bits = plan.tokens, plan.keys, plan.pairs, plan.groups, plan.bits
    vmem = pl.BlockSpec(memory_space=pltpu.VMEM)
    anywhere = pl.BlockSpec(memory_space=pl.ANY)
    names = list(plan.blocks)

    def buf(*shape, dtype=BF):
        return pltpu.VMEM(shape, dtype)

    scratch = [buf(rows, pos, width)] * 4
    scratch += [buf(width, width)] * 4 + [buf(width, hidden), buf(hidden, width)]
    scratch += [
        buf(tokens, width),
        buf(tokens, width, dtype=F32),
        buf(tokens, 1, dtype=F32),
        buf(tokens, width, dtype=F32),
        buf(tokens, 1, dtype=F32),
        buf(tokens, width),
        buf(tokens, width, dtype=F32),
        buf(tokens, width, dtype=F32),
    ]
    scratch += [
        buf(pairs, tokens, PAIR),
        buf(pairs, keys, PAIR),
        buf(pairs, keys, PAIR),
        buf(2 * pairs, tokens, keys, dtype=F32),
        buf(tokens, keys, dtype=F32),
        buf(pairs, tokens, PAIR),
    ]
    scratch += [buf(tokens, hidden), buf(tokens, hidden, dtype=F32), buf(tokens, hidden)]
    scratch += [
        buf(pairs, tokens, PAIR),
        buf(pairs, tokens, PAIR),
        buf(pairs, tokens, PAIR, dtype=F32),
        buf(pairs, tokens, PAIR, dtype=F32),
        buf(2, pairs, keys - plan.far, PAIR, dtype=F32),
    ]
    scratch += [
        buf(2, BLOCK, width),
        buf(groups, 2, BLOCK, width),
        buf(groups, 2, pairs, BLOCK, PAIR),
        buf(groups, 2, pairs, BLOCK, PAIR),
    ]
    head = plan.head
    scratch += [buf(*(2,) * bits, head, *plan.blocks[n]) for n in names]
    for n in names:
        scratch += [buf(*(2,) * (bits - 1 - i), head, *plan.blocks[n]) for i in range(bits)]
    scratch += [buf(head - 1, *plan.blocks[n]) for n in names]
    scratch += [buf(bits + 1, VEC_ROWS, width, dtype=F32), buf(bits + head - 1, VEC_ROWS, width, dtype=F32)]
    dma = pltpu.SemaphoreType.DMA
    scratch += [dma((4, rows)), dma((4, rows)), dma((2, groups)), dma((2, groups))]
    scratch += [dma((7, bits + head - 1)), dma((7, bits + head - 1)), dma((10,))]

    line = lambda a: a.reshape(1, -1)
    results = pl.pallas_call(
        functools.partial(layer_kernel, plan),
        out_shape=[
            jax.ShapeDtypeStruct(inputs.shape, BF),
            jax.ShapeDtypeStruct(inputs.shape, BF),
            *(jax.ShapeDtypeStruct(plan.blocks[n], F32) for n in names),
            jax.ShapeDtypeStruct((VEC_ROWS, width), F32),
        ],
        in_specs=[anywhere, anywhere] + [vmem] * 6 + [anywhere] * 6,
        out_specs=[anywhere, anywhere] + [vmem] * 7,
        scratch_shapes=scratch,
        compiler_params=pltpu.CompilerParams(
            collective_id=0, has_side_effects=True, vmem_limit_bytes=56 << 20
        ),
        name="layer",
    )(
        inputs,
        cotangent,
        line(gain_first),
        line(shift_first),
        line(gain_second),
        line(shift_second),
        line(up_bias),
        line(down_bias),
        query_weight,
        key_weight,
        value_weight,
        out_weight,
        up_weight,
        down_weight,
    )
    layer_out, input_grad, down_g, up_g, out_g, query_g, key_g, value_g, vec = results
    seq_index = lax.axis_index("seq")

    def mine(vector):
        share = vector.shape[0] // plan.seq
        return lax.dynamic_slice_in_dim(vector, seq_index * share, share, 0)

    per = hidden // width
    return (
        layer_out,
        input_grad,
        mine(vec[0]),
        mine(vec[1]),
        query_g,
        key_g,
        value_g,
        out_g,
        mine(vec[2]),
        mine(vec[3]),
        up_g,
        mine(vec[5 : 5 + per].reshape(-1)),
        down_g,
        mine(vec[4]),
    )


def solution(mesh):
    placed = (P(None, ("seq", "head"), None),) + (P(),) * 12 + (P(None, ("seq", "head"), None),)
    return jax.shard_map(
        body,
        mesh=mesh,
        in_specs=placed,
        out_specs=(
            P(None, ("seq", "head"), None),
            P(None, ("seq", "head"), None),
            P("seq"),
            P("seq"),
            P("seq", "head"),
            P("seq", "head"),
            P("seq", "head"),
            P("seq", "head"),
            P("seq"),
            P("seq"),
            P("seq", "head"),
            P("seq"),
            P("seq", "head"),
            P("seq"),
        ),
        check_vma=False,
    )
```

time: 1610 us -> 99 us (0.06); the launches traced: 1580 us -> 98.3 us
  waiting for transfers between devices: 524 us -> 0 us
  local copies, waits for them, and re-layouts: 514 us -> 16 us
  matrix products: 274 us -> 0 us
  other arithmetic: 103 us -> 0 us
  blocking collectives: 95.6 us -> 0 us
  Pallas kernels: 0 us -> 81.6 us
  starting transfers between devices: 51.8 us -> 0 us
  between operations: 22.1 us -> 0.68 us
    reduce_scatter x10 -> x0, waiting for transfers between devices: 459 us -> none  [the longest x3 418 us: body(): lax.psum_scatter(pack_shared(shared_total, seq_count, head_count), ('seq'...]
    dot_general x240 -> x0, matrix products: 274 us -> none  [the longest x56 75.6 us: group_keys(): jnp.einsum('rbmhk,rbmhd->rbkhd', weight_view, left_view, preferred_elemen...]
    reshape x141 -> x0, local copies, waits for them, and re-layouts: 164 us -> none  [the longest x40 58.1 us: group_values(): product.reshape(shape_in[0], shape_in[1], shape_in[2], right.shape[3])]
    all_gather x8 -> x0, blocking collectives: 95.6 us -> none  [the longest x4 59.2 us: body(): x_gathered = lax.all_gather(x_local, 'head', axis=1, tiled=True)]
    pallas_call x0 -> x1, Pallas kernels: none -> 81.6 us  [body(): pl.pallas_call(functools.partial(layer_kernel, plan), out_shape=[jax.Shap...]
    another operation x111 -> x0, local copies, waits for them, and re-layouts: 73.9 us -> none
    transpose x67 -> x0, local copies, waits for them, and re-layouts: 65.4 us -> none  [the longest x32 22.7 us: group_scores(): jnp.einsum('rbmhd,rbkhd->rbmhk', left_view, right_view, preferred_element...]
    unnamed x12 -> x0, waiting for transfers between devices: 52.3 us -> none
  transfers between devices with their start and end apart: 23 -> 0, of which waited for: 11 -> 0; matrix products, arithmetic and copies ran while one was open for 40% -> 0% of each run, Pallas kernels for 0% -> 0%
where the time goes in v1:
time: 99 us; the launch traced here: 98.3 us
  Pallas kernels  81.6 us (82%)
  local copies, waits for them, and re-layouts  16 us (16%)
    pallas_call x1, Pallas kernels, body(): pl.pallas_call(functools.partial(layer_kernel, plan), out_shape=[jax.Shap...  81.6 us
    unnamed x10, local copies, waits for them, and re-layouts  12.7 us
    dynamic_slice x4, local copies, waits for them, and re-layouts, mine(): return lax.dynamic_slice_in_dim(vector, seq_index * share, share, 0)  2.39 us

profile of v1, /device:TPU:0, one launch (start us, length us, event | category | flops | bytes accessed | tf_op | source)
XLA Modules:
  0.0 98.3 jit_solution(8542931817523925483)
XLA Ops:
  0.7 81.6 %layer.1 = (bf16[8,32,512]{2,1,0:T(8,128)(2,1)}, bf16[8,32,512]{2,1,0:T(8,128)(2,1)}, f32[256,128]{1,0:T(8,128)}, f32[64,512]{1,0:T(8,128)}, f32[64,128]{1,0:T(8...) custom-call(bf16[8,32,512]{2,1,0:T(8,128)(2,1)} %refs_0_.1, ...), custom_call_target="tpu_custom_call" | custom-call | tf_op jit(solution)/shard_map/layer/pallas_call | solution.py:678
  82.2 0.9 fusion.5
  83.2 0.6 fusion.2
  83.8 0.6 fusion
  84.3 0.6 fusion.4
  84.9 0.8 slice_bitcast_fusion
  85.7 0.6 dynamic_slice.36
  86.3 1.7 %copy.37 = bf16[8,32,512]{2,1,0:T(8,128)(2,1)} copy(bf16[8,32,512]{2,1,0:T(8,128)(2,1)} %get-tuple-element.55) | data formatting | bytes 524288
  88.0 1.7 %copy.38 = bf16[8,32,512]{2,1,0:T(8,128)(2,1)} copy(bf16[8,32,512]{2,1,0:T(8,128)(2,1)} %get-tuple-element.56) | data formatting | bytes 524288
  89.7 1.4 %copy.39 = f32[64,128]{1,0:T(8,128)} copy(f32[64,128]{1,0:T(8,128)} %get-tuple-element.59) | data formatting | bytes 65536
  91.0 1.4 %copy.40 = f32[64,128]{1,0:T(8,128)} copy(f32[64,128]{1,0:T(8,128)} %get-tuple-element.60) | data formatting | bytes 65536
  92.4 1.4 %copy.41 = f32[64,128]{1,0:T(8,128)} copy(f32[64,128]{1,0:T(8,128)} %get-tuple-element.61) | data formatting | bytes 65536
  93.8 1.4 %copy.42 = f32[64,128]{1,0:T(8,128)} copy(f32[64,128]{1,0:T(8,128)} %get-tuple-element.62) | data formatting | bytes 65536
  95.2 1.6 %copy.43 = f32[64,512]{1,0:T(8,128)} copy(f32[64,512]{1,0:T(8,128)} %get-tuple-element.65) | data formatting | bytes 262144
  96.7 1.6 %copy.44 = f32[256,128]{1,0:T(8,128)} copy(f32[256,128]{1,0:T(8,128)} %get-tuple-element.67) | data formatting | bytes 262144
  (1 shorter events, 0.0 us)

commit v2 on v1

v2 whole, which is shorter than its diff:
```python
import functools

import jax
import jax.numpy as jnp
from jax import lax
from jax.experimental import pallas as pl
from jax.experimental.pallas import tpu as pltpu
from jax.sharding import PartitionSpec as P

MESH = pl.DeviceIdType.MESH
BF = jnp.bfloat16
F32 = jnp.float32
DH = 64
BLOCK = 16
EPSILON = 1e-05
PAIR = 2 * DH
VEC_ROWS = 16


def idiv(value, k):
    return lax.div(value, jnp.int32(k))


def irem(value, k):
    return lax.rem(value, jnp.int32(k))


def bit_of(value, b):
    return irem(idiv(value, 1 << b), 2)


def flip(value, k):
    b = 0
    while k >> b:
        if (k >> b) & 1:
            value = value + (1 - 2 * bit_of(value, b)) * (1 << b)
        b += 1
    return value


def dot(a, b):
    return jnp.dot(a, b, preferred_element_type=F32)


def dot_t(a, b):
    return lax.dot_general(a, b, (((1,), (1,)), ((), ())), preferred_element_type=F32)


def t_dot(a, b):
    return lax.dot_general(a, b, (((0,), (0,)), ((), ())), preferred_element_type=F32)


def two_part_dot(a, b):
    high = b.astype(BF)
    low = (b - high.astype(F32)).astype(BF)
    return dot(a, high) + dot(a, low)


def pair_mean(rows):
    i = lax.broadcasted_iota(jnp.int32, (rows // 2, rows), 0)
    j = lax.broadcasted_iota(jnp.int32, (rows // 2, rows), 1)
    return jnp.where((j >> 1) == i, 0.5, 0.0).astype(BF)


def identity(n):
    i = lax.broadcasted_iota(jnp.int32, (n, n), 0)
    j = lax.broadcasted_iota(jnp.int32, (n, n), 1)
    return jnp.where(i == j, 1.0, 0.0).astype(BF)


def turned(value):
    n = PAIR
    parts = [
        dot_t(identity(n), value[:, i : i + n]).astype(BF) for i in range(0, value.shape[1], n)
    ]
    return parts[0] if len(parts) == 1 else jnp.concatenate(parts, axis=0)


class Plan:
    def __init__(self, seq, head, rows, pos, width, hidden):
        self.seq, self.head, self.rows, self.pos, self.width, self.hidden = seq, head, rows, pos, width, hidden
        self.minor = rows // head
        self.groups = seq // self.minor
        self.tokens = rows * pos
        self.half = self.tokens // 2
        self.pairs = width // PAIR
        self.local = (self.tokens // BLOCK).bit_length() - 1
        self.remote = self.groups.bit_length() - 1
        self.seq_bits = seq.bit_length() - 1
        self.head_bits = head.bit_length() - 1
        self.bits = self.seq_bits + self.head_bits
        self.near = self.half * 2
        self.far = BLOCK * (self.remote - 1)
        cols = width // head
        self.blocks = {
            "down": (hidden // seq, cols),
            "up": (width // seq, hidden // head),
            "out": (width // seq, cols),
            "query": (width // seq, cols),
            "key": (width // seq, cols),
            "value": (width // seq, cols),
        }
        seqs, heads = list(range(self.seq_bits)), list(range(self.seq_bits, self.bits))
        one, two = seqs, seqs[:1] + seqs[:0:-1]

        def cut(name):
            r = self.blocks[name][0]
            m = r // 2 if r % 32 == 0 else r
            return [(name, 0, m)], [(name, m, r)] if m < r else []

        down, up, key = cut("down"), cut("up"), cut("key")
        whole = lambda n: [(n, 0, self.blocks[n][0])]
        self.sums = {
            "down_a": (down[0], one + heads),
            "down_b": (down[1], two + heads),
            "up_a": (up[0], one + heads),
            "up_b": (up[1], two + heads),
            "out": (whole("out"), one[:1] + heads + one[1:]),
            "part_a": (whole("query") + key[0], one + ["head"]),
            "part_b": (key[1] + whole("value"), two + ["head"]),
        }
        self.sums = {n: v for n, v in self.sums.items() if v[0]}

    def sum_shape(self, name):
        parts = self.sums[name][0]
        return (sum(b - a for _, a, b in parts), self.blocks[parts[0][0]][1])

    def got_shapes(self, name):
        left, shapes = self.bits, []
        for b in self.sums[name][1]:
            if b == "head":
                shapes.append((self.head - 1,) + self.sum_shape(name))
            else:
                left -= 1
                shapes.append((2,) * left + self.sum_shape(name))
        return shapes


class Summed:
    def __init__(self, plan, me, name, number, grad, got, send, recv, outs):
        self.plan, self.name, self.number = plan, name, number
        self.s, self.h = me
        self.grad, self.got, self.outs = grad, got, outs
        self.send, self.recv = send, recv
        self.parts, self.order = plan.sums[name]
        self.started, self.stage = [], 0

    def own_bit(self, b):
        n = self.plan.seq_bits
        return bit_of(self.s, b) if b < n else bit_of(self.h, b - n)

    def index(self, fixed, other=None):
        at = []
        for b in reversed(range(self.plan.bits)):
            if b == other:
                at.append(1 - self.own_bit(b))
            elif b in fixed:
                at.append(self.own_bit(b))
            else:
                at.append(slice(None))
        return tuple(at)

    def put(self, name, s, h, block):
        owner = s + h * self.plan.seq
        at = tuple((owner >> b) & 1 for b in reversed(range(self.plan.bits)))
        first = 0
        for part, a, b in self.parts:
            if part == name:
                self.grad[at + (slice(first, first + b - a),)] = block[a:b].astype(BF)
            first += b - a

    def copy(self, source, target, slot, device):
        copy = pltpu.make_async_remote_copy(
            src_ref=source,
            dst_ref=target,
            send_sem=self.send.at[self.number, slot],
            recv_sem=self.recv.at[self.number, slot],
            device_id=device,
            device_id_type=MESH,
        )
        copy.start()
        self.started.append(copy)

    def start(self, stage):
        b = self.order[stage]
        n = self.plan.seq_bits
        if b == "head":
            for k in range(1, self.plan.head):
                peer = flip(self.h, k)
                at = tuple(bit_of(peer, i) for i in reversed(range(self.plan.head_bits)))
                at += self.index(range(n))[self.plan.head_bits :]
                self.copy(self.grad.at[at], self.got[stage].at[k - 1], stage + k - 1, (self.s, peer))
            return
        device = (flip(self.s, 1 << b), self.h) if b < n else (self.s, flip(self.h, 1 << (b - n)))
        source = self.grad.at[self.index(self.order[:stage], b)]
        self.copy(source, self.got[stage], stage, device)

    def finish(self, stage):
        b = self.order[stage]
        if stage + 1 == len(self.order):
            total = self.grad[self.index(range(self.plan.bits))].astype(F32)
            if b == "head":
                for k in range(1, self.plan.head):
                    self.started[stage + k - 1].wait_recv()
                    total = total + self.got[stage][k - 1].astype(F32)
            else:
                self.started[stage].wait_recv()
                total = total + self.got[stage][...].astype(F32)
            first = 0
            for part, a, b in self.parts:
                self.outs[part][a:b, :] = total[first : first + b - a]
                first += b - a
            return
        self.started[stage].wait_recv()
        at = self.index(self.order[: stage + 1])
        combos = [()]
        for a in at:
            if isinstance(a, slice):
                combos = [c + (i,) for c in combos for i in range(2)]
        for combo in combos:
            left = list(combo)
            full = tuple(left.pop(0) if isinstance(a, slice) else a for a in at)
            self.grad[full] = self.grad[full] + self.got[stage][combo]

    def step(self):
        if self.stage:
            self.finish(self.stage - 1)
        if self.stage < len(self.order):
            self.start(self.stage)
        self.stage += 1

    @property
    def done(self):
        return self.stage > len(self.order)

    def drain(self):
        for copy in self.started:
            copy.wait_send()


def layer_kernel(plan, *refs):
    refs = list(refs)

    def take(n):
        taken = refs[:n]
        del refs[:n]
        return taken

    x_in, dy_in, gain_one, shift_one, gain_two, shift_two, up_bias, down_bias = take(8)
    weights_in = take(6)
    lo_out, ig_out = take(2)
    grads_out = dict(zip(plan.blocks, take(6)))
    (vec_out,) = take(1)
    xg, dyg, log, igg = take(4)
    wq, wk, wv, wo, wu, wd = weights = take(6)
    norm_t, n_one, rs_one, n_two, rs_two, norm_two_b, residual, d_residual = take(8)
    qs, kn, vn, kr, vr, kn_t, vn_t, kr_t, vr_t = take(9)
    pn, pr, stats, mask, mixed_t = take(5)
    act_ref, slope_ref, dh_ref = take(3)
    dos, dq_t, dk_ref, dv_ref, far_ref, bar_t = take(6)
    c_send, c_got, d_send, d_got = take(4)
    sums = {}
    for name in plan.sums:
        grad, *got = take(1 + len(plan.sums[name][1]))
        sums[name] = (grad, got)
    vec_bufs, vec_got = take(2)
    send_a, recv_a, send_r, recv_r, send_s, recv_s, here = take(7)
    assert not refs

    seq, head, rows, width, tokens = plan.seq, plan.head, plan.rows, plan.width, plan.tokens
    half, near, far = plan.half, plan.near, plan.far
    s, h = lax.axis_index("seq"), lax.axis_index("head")
    c, g = irem(s, plan.minor), idiv(s, plan.minor)
    j = c * head + h

    def group_peer(k):
        other = flip(j, k)
        return other, (g * plan.minor + idiv(other, head), irem(other, head))

    def row_peer(k):
        other = flip(g, k)
        return other, (other * plan.minor + c, h)

    barrier = pltpu.get_barrier_semaphore()
    peers = [group_peer(k)[1] for k in range(1, rows)] + [row_peer(k)[1] for k in range(1, plan.groups)]
    for device in peers:
        pl.semaphore_signal(barrier, inc=1, device_id=device, device_id_type=MESH)

    loads = [pltpu.make_async_copy(a, b, here.at[i]) for i, (a, b) in enumerate(zip(weights_in, weights))]
    for i in (1, 2, 0, 3, 4, 5):
        loads[i].start()
    own = [
        pltpu.make_async_copy(x_in.at[j], xg.at[j], here.at[6]),
        pltpu.make_async_copy(dy_in.at[j], dyg.at[j], here.at[7]),
    ]
    for copy in own:
        copy.start()

    i_k = lax.broadcasted_iota(jnp.int32, (near, 2 * half), 0)
    i_q = lax.broadcasted_iota(jnp.int32, (near, 2 * half), 1) & (half - 1)
    valid = (i_k < half) & ((i_q >> 5) == (i_k >> 5))
    first = half
    for level in range(1, plan.local - 1):
        count = half >> level
        mine = (i_k >= first) & (i_k < first + count)
        valid = valid | (mine & (((i_q >> (4 + level)) ^ 1) == ((i_k - first) >> 4)))
        first += count
    valid = valid | (i_k >= first)
    mask[...] = jnp.where(valid, 0.0, -1e30).astype(F32)

    pl.semaphore_wait(barrier, len(peers))

    def exchange(number, source, target):
        copies = []
        for k in range(1, rows):
            other, device = group_peer(k)
            copy = pltpu.make_async_remote_copy(
                src_ref=source.at[other],
                dst_ref=target.at[j],
                send_sem=send_a.at[number, k],
                recv_sem=recv_a.at[number, k],
                device_id=device,
                device_id_type=MESH,
            )
            copy.start()
            copies.append(copy)
        return copies

    x_copies = exchange(0, x_in, xg)

    def norm_stats(values):
        center = values - jnp.mean(values, axis=-1, keepdims=True)
        spread = jnp.mean(center * center, axis=-1, keepdims=True)
        scale = lax.rsqrt(spread + EPSILON)
        return center * scale, scale

    def norm_back(d_norm, n, scale, gain):
        weighted = d_norm * gain
        return scale * (
            weighted
            - jnp.mean(weighted, axis=-1, keepdims=True)
            - n * jnp.mean(weighted * n, axis=-1, keepdims=True)
        )

    lane = lax.broadcasted_iota(jnp.int32, (1, PAIR), 1)
    low = lane < DH

    def stack_heads(ref, value):
        for p in range(plan.pairs):
            for a in range(2):
                part = value[a * half : (a + 1) * half, p * PAIR : (p + 1) * PAIR]
                zero = jnp.zeros_like(part)
                ref[p, a, :half, :] = jnp.where(low, part, zero)
                ref[p, a, half:, :] = jnp.where(low, zero, part)

    own[0].wait()
    for copy in x_copies:
        copy.wait_recv()
    dy_copies = exchange(1, dy_in, dyg)
    x = xg[...].reshape(tokens, width).astype(F32)
    n, scale = norm_stats(x)
    n_one[...] = n
    rs_one[...] = scale
    normed = (n * gain_one[...] + shift_one[...]).astype(BF)

    loads[1].wait()
    loads[2].wait()
    level = jnp.concatenate([dot(normed, wk[...]).astype(BF), dot(normed, wv[...]).astype(BF)], axis=1)

    def columns(index, p):
        return slice(index * width + p * PAIR, index * width + (p + 1) * PAIR)

    targets = (kn, vn)
    first = 0
    for l in range(plan.local):
        if l:
            level = dot(pair_mean(level.shape[0]), level).astype(BF)
        count = level.shape[0] // 2
        for index, ref in enumerate(targets):
            for p in range(plan.pairs):
                for a in range(2):
                    b = a if l + 1 < plan.local else 1 - a
                    ref[p, b, first : first + count, :] = level[a * count : (a + 1) * count, columns(index, p)]
        first += count
    level = dot(pair_mean(level.shape[0]), level).astype(BF)
    c_send[0] = level[:, :width]
    c_send[1] = level[:, width:]
    i_a = lax.broadcasted_iota(jnp.int32, (BLOCK, tokens), 0)
    i_b = lax.broadcasted_iota(jnp.int32, (BLOCK, tokens), 1)
    mean_all = jnp.where((i_b >> plan.local) == i_a, 0.5**plan.local, 0.0).astype(BF)
    c_send[2] = dot(mean_all, normed).astype(BF)
    c_copies = []
    for k in range(1, plan.groups):
        other, device = row_peer(k)
        copy = pltpu.make_async_remote_copy(
            src_ref=c_send,
            dst_ref=c_got.at[g],
            send_sem=send_r.at[0, k],
            recv_sem=recv_r.at[0, k],
            device_id=device,
            device_id_type=MESH,
        )
        copy.start()
        c_copies.append(copy)

    loads[0].wait()
    stack_heads(qs, (dot(normed, wq[...]) * (DH**-0.5)).astype(BF))
    norm_t[...] = turned(normed)
    local = near - BLOCK

    def attend_near(p, carry):
        for a in range(2):
            scores = dot_t(kn[p, a, :local, :], qs[p, a]) + mask[:local, :]
            top = jnp.max(scores, axis=0, keepdims=True)
            raised = jnp.exp(scores - top)
            pn[p, a, :local, :] = raised
            stats[p, a, 0:1, :] = top
            stats[p, a, 1:2, :] = jnp.sum(raised, axis=0, keepdims=True)
        return carry

    lax.fori_loop(0, plan.pairs, attend_near, 0)

    for copy in c_copies:
        copy.wait_recv()
    for index in range(3):
        for b in range(plan.remote):
            upper = idiv(g, 1 << b)
            base = (upper + 1 - 2 * irem(upper, 2)) * (1 << b)
            level = c_got[pl.ds(base, 1 << b), index].reshape(BLOCK << b, width)
            for _ in range(b):
                level = dot(pair_mean(level.shape[0]), level).astype(BF)
            if index == 2:
                bar_t[:, b * BLOCK : (b + 1) * BLOCK] = turned(level)
                continue
            for p in range(plan.pairs):
                part = level[:, p * PAIR : (p + 1) * PAIR]
                if b == 0:
                    for a in range(2):
                        targets[index][p, a, local:, :] = part
                else:
                    (kr, vr)[index][p, (b - 1) * BLOCK : b * BLOCK, :] = part

    def attend(p, carry):
        kr_t[p] = turned(kr[p])
        vr_t[p] = turned(vr[p])
        for a in range(2):
            kn_t[p, a] = turned(kn[p, a])
            vn_t[p, a] = turned(vn[p, a])
            q = qs[p, a]
            top_near = stats[p, a, 0:1, :]
            first_far = dot_t(kn[p, a, local:, :], q)
            rest_far = dot_t(kr[p], q)
            top = jnp.maximum(
                top_near,
                jnp.maximum(
                    jnp.max(first_far, axis=0, keepdims=True), jnp.max(rest_far, axis=0, keepdims=True)
                ),
            )
            shrink = jnp.exp(top_near - top)
            first_far = jnp.exp(first_far - top)
            rest_far = jnp.exp(rest_far - top)
            total = (
                stats[p, a, 1:2, :] * shrink
                + jnp.sum(first_far, axis=0, keepdims=True)
                + jnp.sum(rest_far, axis=0, keepdims=True)
            )
            share = 1.0 / total
            pn[p, a, :local, :] = pn[p, a, :local, :] * (shrink * share)
            pn[p, a, local:, :] = first_far * share
            rest_far = rest_far * share
            pr[p, a] = rest_far
            mixed = dot(vn_t[p, a], pn[p, a].astype(BF)) + dot(vr_t[p], rest_far.astype(BF))
            mixed_t[p, :DH, a * half : (a + 1) * half] = mixed[:DH, :half].astype(BF)
            mixed_t[p, DH:, a * half : (a + 1) * half] = mixed[DH:, half:].astype(BF)
        return carry

    lax.fori_loop(0, plan.pairs, attend, 0)

    loads[3].wait()
    res = xg[...].reshape(tokens, width).astype(F32) + t_dot(mixed_t[...].reshape(width, tokens), wo[...])
    residual[...] = res
    n, scale = norm_stats(res)
    n_two[...] = n
    rs_two[...] = scale
    norm_two_b[...] = (n * gain_two[...] + shift_two[...]).astype(BF)

    sums = {
        name: Summed(plan, (s, h), name, i, grad, got, send_s, recv_s, grads_out)
        for i, (name, (grad, got)) in enumerate(sums.items())
    }
    row = lambda a: jnp.sum(a, axis=0, keepdims=True)

    def step(*names):
        for name in names:
            if name in sums:
                sums[name].step()

    def put_all(name, block, first_row, first_col):
        r, w = plan.blocks[name]
        for a in range(0, block.shape[0], r):
            for b in range(0, block.shape[1], w):
                for item in sums.values():
                    item.put(name, (first_row + a) // r, (first_col + b) // w, block[a : a + r, b : b + w])

    loads[4].wait()
    loads[5].wait()
    own[1].wait()
    for copy in dy_copies:
        copy.wait_recv()
    chunk = 512
    dy = dyg[...].reshape(tokens, width)
    for f in range(0, plan.hidden, chunk):
        hid = dot(norm_two_b[...], wu[:, f : f + chunk]) + up_bias[:, f : f + chunk]
        cdf = 0.5 * (1.0 + lax.erf(hid * (0.5**0.5)))
        act = (hid * cdf).astype(BF)
        act_ref[:, f : f + chunk] = act
        slope_ref[:, f : f + chunk] = cdf + hid * (jnp.exp(-0.5 * hid * hid) * 0.3989422804014327)
        put_all("down", t_dot(act, dy), f, 0)
    step("down_a", "down_b")

    hidden_rows = []
    for i, f in enumerate(range(0, plan.hidden, chunk)):
        dh = (dot_t(dy, wd[f : f + chunk, :]) * slope_ref[:, f : f + chunk]).astype(BF)
        dh_ref[:, f : f + chunk] = dh
        hidden_rows.append(row(dh.astype(F32)))
        put_all("up", t_dot(norm_two_b[...], dh), 0, f)
        if i == 2:
            step("down_a", "down_b")
    step("up_a", "up_b")

    d_norm_two = dot_t(dh_ref[...], wu[...])
    n = n_two[...]
    dy_f = dy.astype(F32)
    vec_bufs[0, 2:3, :] = row(d_norm_two * n)
    vec_bufs[0, 3:4, :] = row(d_norm_two)
    vec_bufs[0, 4:5, :] = row(dy_f)
    per = plan.hidden // width
    flat = jnp.concatenate(hidden_rows, axis=1)
    for i in range(per):
        vec_bufs[0, 5 + i : 6 + i, :] = flat[:, i * width : (i + 1) * width]
    d_res = dy_f + norm_back(d_norm_two, n, rs_two[...], gain_two[...])
    d_residual[...] = d_res
    d_mix = d_res.astype(BF)
    step("up_a", "up_b")
    put_all("out", dot(mixed_t[...].reshape(width, tokens), d_mix), 0, 0)
    step("out")
    stack_heads(dos, dot_t(d_mix, wo[...]).astype(BF))

    i_t = lax.broadcasted_iota(jnp.int32, (half, half), 0)
    i_c = lax.broadcasted_iota(jnp.int32, (half, half), 1)
    spread = jnp.zeros((half, half), F32)
    first = 0
    for level in range(1, plan.local):
        spread = spread + jnp.where((i_t >> level) == (i_c - first), 0.5**level, 0.0)
        first += half >> level
    spread = jnp.where(i_c < first, spread, 0.0).astype(BF)

    def attend_back(p, carry):
        dk, dv, dk_far, dv_far = [], [], 0.0, 0.0
        for a in range(2):
            q, do = qs[p, a], dos[p, a]
            prob, prob_far = pn[p, a], pr[p, a]
            d_prob = dot_t(vn[p, a], do)
            d_prob_far = dot_t(vr[p], do)
            inner = row(prob * d_prob) + row(prob_far * d_prob_far)
            d_scores = (prob * (d_prob - inner)).astype(BF)
            d_scores_far = (prob_far * (d_prob_far - inner)).astype(BF)
            dk.append(dot(d_scores, q))
            dv.append(dot(prob.astype(BF), do))
            dk_far = dk_far + dot(d_scores_far, q)
            dv_far = dv_far + dot(prob_far.astype(BF), do)
            dq = (dot(kn_t[p, a], d_scores) + dot(kr_t[p], d_scores_far)) * (DH**-0.5)
            dq_t[p, :DH, a * half : (a + 1) * half] = dq[:DH, :half].astype(BF)
            dq_t[p, DH:, a * half : (a + 1) * half] = dq[DH:, half:].astype(BF)
        other = half + first - BLOCK
        for index, (total, total_far, ref) in enumerate(((dk, dk_far, dk_ref), (dv, dv_far, dv_ref))):
            for a in range(2):
                coarse = jnp.concatenate(
                    [total[a][half:other], total[1 - a][other : other + BLOCK], total[a][local:]], axis=0
                )
                ref[p, a * half : (a + 1) * half, :] = total[a][:half] + two_part_dot(spread, coarse)
            far_ref[index, p, :BLOCK, :] = total[0][local:] + total[1][local:]
            far_ref[index, p, BLOCK:, :] = total_far
        return carry

    lax.fori_loop(0, plan.pairs // 2, attend_back, 0)

    result = residual[...] + dot(act_ref[...], wd[...]) + down_bias[...]
    log[...] = result.astype(BF).reshape(rows, plan.pos, width)
    lo_copies = exchange(2, log, lo_out)
    lo_own = pltpu.make_async_copy(log.at[j], lo_out.at[j], here.at[8])
    lo_own.start()
    step("out")

    lax.fori_loop(plan.pairs // 2, plan.pairs, attend_back, 0)

    i_a = lax.broadcasted_iota(jnp.int32, (BLOCK, BLOCK), 0)
    i_b = lax.broadcasted_iota(jnp.int32, (BLOCK, BLOCK), 1)
    d_copies = []
    for k in range(1, plan.groups):
        other, device = row_peer(k)
        b = k.bit_length() - 1
        offset = irem(other, 1 << b)
        pick = jnp.where(((offset * BLOCK + i_a) >> b) == i_b, 0.5**b, 0.0).astype(BF)
        for index in range(2):
            for p in range(plan.pairs):
                level = far_ref[index, p, BLOCK * b : BLOCK * (b + 1), :].astype(BF)
                d_send[k, index, p] = dot(pick, level).astype(BF)
        copy = pltpu.make_async_remote_copy(
            src_ref=d_send.at[k],
            dst_ref=d_got.at[k],
            send_sem=send_r.at[1, k],
            recv_sem=recv_r.at[1, k],
            device_id=device,
            device_id_type=MESH,
        )
        copy.start()
        d_copies.append(copy)

    d_query_t = dq_t[...].reshape(width, tokens)
    put_all("query", dot_t(norm_t[...], d_query_t), 0, 0)
    for index, (ref, name) in enumerate(((dk_ref, "key"), (dv_ref, "value"))):
        mine = jnp.concatenate([ref[p].astype(BF) for p in range(plan.pairs)], axis=1)
        made = jnp.concatenate([far_ref[index, p].astype(BF) for p in range(plan.pairs)], axis=1)
        put_all(name, dot(norm_t[...], mine) + dot(bar_t[...], made), 0, 0)
        if name == "key":
            step("part_a")
    step("part_b")
    step("down_a", "down_b")
    d_normed = dot_t(turned(d_query_t), wq[...])
    step("part_a", "part_b", "out")

    for copy in d_copies:
        copy.wait_recv()
    i_t = lax.broadcasted_iota(jnp.int32, (tokens, BLOCK), 0)
    i_c = lax.broadcasted_iota(jnp.int32, (tokens, BLOCK), 1)
    last = jnp.where((i_t >> plan.local) == i_c, 0.5**plan.local, 0.0).astype(BF)
    for index, (ref, w) in enumerate(((dk_ref, wk), (dv_ref, wv))):
        pieces = []
        for p in range(plan.pairs):
            coarse = d_got[1, index, p].astype(F32)
            for k in range(2, plan.groups):
                coarse = coarse + d_got[k, index, p].astype(F32)
            pieces.append((ref[p] + two_part_dot(last, coarse)).astype(BF))
        d_normed = d_normed + dot_t(jnp.concatenate(pieces, axis=1), w[...])
    n = n_one[...]
    vec_bufs[0, 0:1, :] = row(d_normed * n)
    vec_bufs[0, 1:2, :] = row(d_normed)
    vec_bufs[0, 5 + per :, :] = jnp.zeros((VEC_ROWS - 5 - per, width), F32)
    d_first = norm_back(d_normed, n, rs_one[...], gain_one[...])
    igg[...] = (d_residual[...] + d_first).astype(BF).reshape(rows, plan.pos, width)

    vec_copies = []

    def vec_start(stage):
        if stage < plan.seq_bits:
            jobs = [(stage, (flip(s, 1 << stage), h))]
        else:
            jobs = [(plan.seq_bits + k - 1, (s, flip(h, k))) for k in range(1, head)]
        for slot, device in jobs:
            copy = pltpu.make_async_remote_copy(
                src_ref=vec_bufs.at[stage],
                dst_ref=vec_got.at[slot],
                send_sem=send_s.at[len(plan.sums), slot],
                recv_sem=recv_s.at[len(plan.sums), slot],
                device_id=device,
                device_id_type=MESH,
            )
            copy.start()
            vec_copies.append(copy)

    def vec_finish(stage):
        vec_copies[stage].wait_recv()
        vec_bufs[stage + 1] = vec_bufs[stage] + vec_got[stage]

    vec_start(0)
    ig_copies = exchange(3, igg, ig_out)
    ig_own = pltpu.make_async_copy(igg.at[j], ig_out.at[j], here.at[9])
    ig_own.start()

    stage = 0
    while stage < plan.seq_bits or not all(item.done for item in sums.values()):
        for name in ("up_a", "up_b", "down_a", "down_b", "part_a", "part_b", "out"):
            if name in sums and not sums[name].done:
                sums[name].step()
        if stage < plan.seq_bits:
            vec_finish(stage)
            vec_start(stage + 1)
        stage += 1
    values = [vec_bufs[plan.seq_bits]]
    for k in range(1, head):
        vec_copies[plan.seq_bits + k - 1].wait_recv()
        values.append(vec_got[plan.seq_bits + k - 1])
    while len(values) > 1:
        values = [values[i] + values[i + 1] for i in range(0, len(values), 2)]
    vec = values[0]

    def own_part(line):
        share = line.shape[1] // seq
        part = line[:, :share]
        for other in range(1, seq):
            part = jnp.where(s == other, line[:, other * share : (other + 1) * share], part)
        return part

    vec_out[...] = jnp.zeros_like(vec_out)
    part = own_part(vec[:8])
    vec_out[:, : part.shape[1]] = part
    part = own_part(jnp.concatenate([vec[5 + i : 6 + i] for i in range(per)], axis=1))
    vec_out[5:6, : part.shape[1]] = part

    for copy in lo_copies + ig_copies:
        copy.wait_recv()
    lo_own.wait()
    ig_own.wait()
    for copy in x_copies + dy_copies + lo_copies + ig_copies + c_copies + d_copies + vec_copies:
        copy.wait_send()
    for item in sums.values():
        item.drain()


def place_kernel(*refs):
    ins, outs, sems = refs[:9], refs[9:-1], refs[-1]
    vec, lines = ins[-1], outs[8:]
    copies = [pltpu.make_async_copy(ins[i], outs[i], sems.at[i]) for i in range(8)]
    for copy in copies:
        copy.start()
    for i, line in enumerate(lines):
        line[...] = vec[i, : line.shape[0]]
    for copy in copies:
        copy.wait()


def body(
    inputs,
    gain_first,
    shift_first,
    query_weight,
    key_weight,
    value_weight,
    out_weight,
    gain_second,
    shift_second,
    up_weight,
    up_bias,
    down_weight,
    down_bias,
    cotangent,
):
    rows, pos, width = inputs.shape
    hidden = up_weight.shape[1]
    plan = Plan(lax.axis_size("seq"), lax.axis_size("head"), rows, pos, width, hidden)
    tokens, pairs, groups, half, near, far = plan.tokens, plan.pairs, plan.groups, plan.half, plan.near, plan.far
    vmem = pl.BlockSpec(memory_space=pltpu.VMEM)
    anywhere = pl.BlockSpec(memory_space=pl.ANY)
    names = list(plan.blocks)

    def buf(*shape, dtype=BF):
        return pltpu.VMEM(shape, dtype)

    scratch = [buf(rows, pos, width)] * 4
    scratch += [buf(width, width)] * 4 + [buf(width, hidden), buf(hidden, width)]
    scratch += [
        buf(width, tokens),
        buf(tokens, width, dtype=F32),
        buf(tokens, 1, dtype=F32),
        buf(tokens, width, dtype=F32),
        buf(tokens, 1, dtype=F32),
        buf(tokens, width),
        buf(tokens, width, dtype=F32),
        buf(tokens, width, dtype=F32),
    ]
    scratch += [
        buf(pairs, 2, tokens, PAIR),
        buf(pairs, 2, near, PAIR),
        buf(pairs, 2, near, PAIR),
        buf(pairs, far, PAIR),
        buf(pairs, far, PAIR),
        buf(pairs, 2, PAIR, near),
        buf(pairs, 2, PAIR, near),
        buf(pairs, PAIR, far),
        buf(pairs, PAIR, far),
    ]
    scratch += [
        buf(pairs, 2, near, tokens, dtype=F32),
        buf(pairs, 2, far, tokens, dtype=F32),
        buf(pairs, 2, 8, tokens, dtype=F32),
        buf(near, tokens, dtype=F32),
        buf(pairs, PAIR, tokens),
    ]
    scratch += [buf(tokens, hidden), buf(tokens, hidden, dtype=F32), buf(tokens, hidden)]
    scratch += [
        buf(pairs, 2, tokens, PAIR),
        buf(pairs, PAIR, tokens),
        buf(pairs, tokens, PAIR, dtype=F32),
        buf(pairs, tokens, PAIR, dtype=F32),
        buf(2, pairs, BLOCK * plan.remote, PAIR, dtype=F32),
        buf(width, BLOCK * plan.remote),
    ]
    scratch += [
        buf(3, BLOCK, width),
        buf(groups, 3, BLOCK, width),
        buf(groups, 2, pairs, BLOCK, PAIR),
        buf(groups, 2, pairs, BLOCK, PAIR),
    ]
    for name in plan.sums:
        scratch += [buf(*(2,) * plan.bits, *plan.sum_shape(name))]
        scratch += [buf(*shape) for shape in plan.got_shapes(name)]
    slots = plan.bits + plan.head
    scratch += [
        buf(plan.seq_bits + 1, VEC_ROWS, width, dtype=F32),
        buf(plan.seq_bits + plan.head - 1, VEC_ROWS, width, dtype=F32),
    ]
    dma = pltpu.SemaphoreType.DMA
    scratch += [dma((4, rows)), dma((4, rows)), dma((2, groups)), dma((2, groups))]
    scratch += [dma((len(plan.sums) + 1, slots)), dma((len(plan.sums) + 1, slots)), dma((10,))]

    line = lambda a: a.reshape(1, -1)
    big = [jax.ShapeDtypeStruct(inputs.shape, BF)] * 2 + [jax.ShapeDtypeStruct(plan.blocks[n], F32) for n in names]
    share = max(width, hidden) // plan.seq
    results = pl.pallas_call(
        functools.partial(layer_kernel, plan),
        out_shape=big + [jax.ShapeDtypeStruct((8, share), F32)],
        in_specs=[anywhere, anywhere] + [vmem] * 6 + [anywhere] * 6,
        out_specs=[anywhere, anywhere] + [vmem] * 7,
        scratch_shapes=scratch,
        compiler_params=pltpu.CompilerParams(
            collective_id=0, has_side_effects=True, vmem_limit_bytes=56 << 20
        ),
        name="layer",
    )(
        inputs,
        cotangent,
        line(gain_first),
        line(shift_first),
        line(gain_second),
        line(shift_second),
        line(up_bias),
        line(down_bias),
        query_weight,
        key_weight,
        value_weight,
        out_weight,
        up_weight,
        down_weight,
    )
    lines = [jax.ShapeDtypeStruct((width // plan.seq,), F32)] * 5 + [jax.ShapeDtypeStruct((hidden // plan.seq,), F32)]
    placed = pl.pallas_call(
        place_kernel,
        out_shape=big + lines,
        in_specs=[anywhere] * 8 + [vmem],
        out_specs=[vmem] * 14,
        scratch_shapes=[dma((8,))],
        name="place",
    )(*results)
    layer_out, input_grad, down_g, up_g, out_g, query_g, key_g, value_g = placed[:8]
    gain_one_g, shift_one_g, gain_two_g, shift_two_g, down_bias_g, up_bias_g = placed[8:]
    return (
        layer_out,
        input_grad,
        gain_one_g,
        shift_one_g,
        query_g,
        key_g,
        value_g,
        out_g,
        gain_two_g,
        shift_two_g,
        up_g,
        up_bias_g,
        down_g,
        down_bias_g,
    )


def solution(mesh):
    placed = (P(None, ("seq", "head"), None),) + (P(),) * 12 + (P(None, ("seq", "head"), None),)
    return jax.shard_map(
        body,
        mesh=mesh,
        in_specs=placed,
        out_specs=(
            P(None, ("seq", "head"), None),
            P(None, ("seq", "head"), None),
            P("seq"),
            P("seq"),
            P("seq", "head"),
            P("seq", "head"),
            P("seq", "head"),
            P("seq", "head"),
            P("seq"),
            P("seq"),
            P("seq", "head"),
            P("seq"),
            P("seq", "head"),
            P("seq"),
        ),
        check_vma=False,
    )
```

time: 99 us -> 75 us (0.76)
  local copies, waits for them, and re-layouts: 16 us -> 0 us
  Pallas kernels: 81.6 us -> 74.1 us
    unnamed x10 -> x0, local copies, waits for them, and re-layouts: 12.7 us -> none
    pallas_call x1 -> x2, Pallas kernels: 81.6 us -> 74.1 us  [the longest x1 71.3 us: body(): pl.pallas_call(functools.partial(layer_kernel, plan), out_shape=big + [ja...]
    dynamic_slice x4 -> x0, local copies, waits for them, and re-layouts: 2.39 us -> none  [mine(): return lax.dynamic_slice_in_dim(vector, seq_index * share, share, 0)]
where the time goes in v2:
time: 75 us; the launch traced here: 74.8 us
  Pallas kernels  74.1 us (99%)
    pallas_call x1, Pallas kernels, body(): pl.pallas_call(functools.partial(layer_kernel, plan), out_shape=big + [ja...  71.3 us
    pallas_call x1, Pallas kernels, body(): pl.pallas_call(place_kernel, out_shape=big + lines, in_specs=[anywhere] *...  2.81 us

profile of v2, /device:TPU:0, one launch (start us, length us, event | category | flops | bytes accessed | tf_op | source)
XLA Modules:
  0.0 74.8 jit_solution(12626252270011681594)
XLA Ops:
  0.7 71.3 %layer.1 = (bf16[8,32,512]{2,1,0:T(8,128)(2,1)}, bf16[8,32,512]{2,1,0:T(8,128)(2,1)}, f32[256,128]{1,0:T(8,128)}, f32[64,512]{1,0:T(8,128)}, f32[64,128]{1,0:T(8...) custom-call(bf16[8,32,512]{2,1,0:T(8,128)(2,1)} %refs_0_.1, ...), custom_call_target="tpu_custom_call" | custom-call | tf_op jit(solution)/shard_map/layer/pallas_call | solution.py:820
  72.0 2.8 %place.1 = (bf16[8,32,512]{2,1,0:T(8,128)(2,1)}, bf16[8,32,512]{2,1,0:T(8,128)(2,1)}, f32[256,128]{1,0:T(8,128)}, f32[64,512]{1,0:T(8,128)}, f32[64,128]{1,0:T(8...) custom-call(bf16[8,32,512]{2,1,0:T(8,128)(2,1)} %get-tuple-element.3, ...), custom_call_target="tpu_custom_call" | custom-call | tf_op jit(solution)/shard_map/place/pallas_call | solution.py:847

commit v3 on v2

--- a/solution.py
+++ b/solution.py
@@ -15,6 +15,25 @@
 EPSILON = 1e-05
 PAIR = 2 * DH
 VEC_ROWS = 16
+LANES = 128
+ORDER = (
+    "ffn1a", "dna", "ffn1b", "Abar", "dnb", "dnc", "dna", "ffn2a", "upa", "dnc", "dnb", "ffn2b", "lo", "Alo",
+    "upb", "ln2b", "outg", "upa", "dmix", "bar", "upb", "ab0", "ab1", "dnb", "dnc", "outa", "outa", "ab2",
+    "ab3", "dna", "dsend", "qkvg", "dnb", "outa", "upb", "dnq", "pa", "pb", "upa", "dnb", "pb", "dnc", "dna",
+    "Wd", "ln1b", "vec", "pa", "upb", "dnc", "upa", "Aig", "dna", "vec", "outa", "pb", "outa", "vec", "upb",
+    "dnc", "dnb", "upa", "pa", "pb", "vec", "pa", "upa", "vec", "outa", "pa", "pb", "upb",
+)
+STAGES = {
+    "dna": ("straight", "head"),
+    "dnb": ("back", "bits"),
+    "dnc": ("bits", "straight"),
+    "upa": ("straight", "bits"),
+    "upb": ("back", "bits"),
+    "outa": ("bits", "straight"),
+    "pa": ("straight", "head"),
+    "pb": ("back", "head"),
+}
+EIGHTHS = 2
 
 
 def idiv(value, k):
@@ -101,29 +120,53 @@
             "value": (width // seq, cols),
         }
         seqs, heads = list(range(self.seq_bits)), list(range(self.seq_bits, self.bits))
-        one, two = seqs, seqs[:1] + seqs[:0:-1]
-
-        def cut(name):
-            r = self.blocks[name][0]
-            m = r // 2 if r % 32 == 0 else r
-            return [(name, 0, m)], [(name, m, r)] if m < r else []
-
-        down, up, key = cut("down"), cut("up"), cut("key")
-        whole = lambda n: [(n, 0, self.blocks[n][0])]
-        self.sums = {
-            "down_a": (down[0], one + heads),
-            "down_b": (down[1], two + heads),
-            "up_a": (up[0], one + heads),
-            "up_b": (up[1], two + heads),
-            "out": (whole("out"), one[:1] + heads + one[1:]),
-            "part_a": (whole("query") + key[0], one + ["head"]),
-            "part_b": (key[1] + whole("value"), two + ["head"]),
-        }
-        self.sums = {n: v for n, v in self.sums.items() if v[0]}
+        ways = {"core": seqs[:1], "straight": seqs[1:], "back": seqs[:0:-1], "bits": heads, "head": ["head"]}
+        stages = {name: [b for way in ("core",) + STAGES[name] for b in ways[way]] for name in STAGES}
+        rows_down, rows_up, rows_out = hidden // seq, width // seq, width // seq
+        self.fine = rows_down % (2 * LANES) == 0
+        half_down = rows_down // 2
+        if self.fine:
+            self.chunks = [
+                [(s * rows_down + i * half_down, half_down) for s in range(seq)] for i in range(2)
+            ]
+        else:
+            self.chunks = [[(0, hidden)], []]
+
+        def tall(name, *cuts):
+            return [(name, r, r + n, c, c + LANES) for r, n in cuts for c in range(0, self.blocks[name][1], LANES)]
+
+        if self.fine:
+            third = half_down // 8 * EIGHTHS
+            step = 2 * half_down
+            first = [(c, c + half_down) for c in range(0, hidden // head, step)]
+            second = [(c + half_down, c + step) for c in range(0, hidden // head, step)]
+            lanes = lambda cs: [("up", 0, rows_up, c, c + LANES) for a, b in cs for c in range(a, b, LANES)]
+            self.sums = {
+                "dna": (tall("down", (0, half_down - third)), stages["dna"]),
+                "dnb": (tall("down", (half_down, half_down - third)), stages["dnb"]),
+                "dnc": (
+                    tall("down", (half_down - third, third), (2 * half_down - third, third)),
+                    stages["dnc"],
+                ),
+                "upa": (lanes(first), stages["upa"]),
+                "upb": (lanes(second), stages["upb"]),
+            }
+        else:
+            self.sums = {
+                "dna": (tall("down", (0, rows_down)), stages["dna"]),
+                "upb": (tall("up", (0, rows_up)), stages["upb"]),
+            }
+        self.sums["outa"] = (tall("out", (0, rows_out)), stages["outa"])
+        if rows_out % 32 == 0:
+            m = rows_out // 2
+            self.sums["pa"] = (tall("query", (0, rows_out)) + tall("key", (0, m)), stages["pa"])
+            self.sums["pb"] = (tall("key", (m, m)) + tall("value", (0, rows_out)), stages["pb"])
+        else:
+            self.sums["pa"] = (tall("query", (0, rows_out)) + tall("key", (0, rows_out)), stages["pa"])
+            self.sums["pb"] = (tall("value", (0, rows_out)), stages["pb"])
 
     def sum_shape(self, name):
-        parts = self.sums[name][0]
-        return (sum(b - a for _, a, b in parts), self.blocks[parts[0][0]][1])
+        return (sum(part[2] - part[1] for part in self.sums[name][0]), LANES)
 
     def got_shapes(self, name):
         left, shapes = self.bits, []
@@ -160,14 +203,15 @@
                 at.append(slice(None))
         return tuple(at)
 
-    def put(self, name, s, h, block):
+    def put(self, name, s, h, block, row, col):
         owner = s + h * self.plan.seq
         at = tuple((owner >> b) & 1 for b in reversed(range(self.plan.bits)))
         first = 0
-        for part, a, b in self.parts:
-            if part == name:
-                self.grad[at + (slice(first, first + b - a),)] = block[a:b].astype(BF)
-            first += b - a
+        for part, r0, r1, c0, c1 in self.parts:
+            if part == name and row <= r0 < row + block.shape[0] and col <= c0 < col + block.shape[1]:
+                piece = block[r0 - row : r1 - row, c0 - col : c1 - col]
+                self.grad[at + (slice(first, first + r1 - r0),)] = piece.astype(BF)
+            first += r1 - r0
 
     def copy(self, source, target, slot, device):
         copy = pltpu.make_async_remote_copy(
@@ -207,9 +251,9 @@
                 self.started[stage].wait_recv()
                 total = total + self.got[stage][...].astype(F32)
             first = 0
-            for part, a, b in self.parts:
-                self.outs[part][a:b, :] = total[first : first + b - a]
-                first += b - a
+            for part, r0, r1, c0, c1 in self.parts:
+                self.outs[part][r0:r1, c0:c1] = total[first : first + r1 - r0]
+                first += r1 - r0
             return
         self.started[stage].wait_recv()
         at = self.index(self.order[: stage + 1])
@@ -246,24 +290,25 @@
         del refs[:n]
         return taken
 
-    x_in, dy_in, gain_one, shift_one, gain_two, shift_two, up_bias, down_bias = take(8)
+    x_in, dy_in, *lines_in = take(8)
     weights_in = take(6)
     lo_out, ig_out = take(2)
     grads_out = dict(zip(plan.blocks, take(6)))
-    (vec_out,) = take(1)
+    lines_out = take(6)
     xg, dyg, log, igg = take(4)
     wq, wk, wv, wo, wu, wd = weights = take(6)
+    gain_one, shift_one, gain_two, shift_two, up_bias, down_bias = lines = take(6)
     norm_t, n_one, rs_one, n_two, rs_two, norm_two_b, residual, d_residual = take(8)
     qs, kn, vn, kr, vr, kn_t, vn_t, kr_t, vr_t = take(9)
     pn, pr, stats, mask, mixed_t = take(5)
-    act_ref, slope_ref, dh_ref = take(3)
-    dos, dq_t, dk_ref, dv_ref, far_ref, bar_t = take(6)
-    c_send, c_got, d_send, d_got = take(4)
+    act_ref, hid_ref, cdf_ref, dh_ref = take(4)
+    dos, dq_t, dk_ref, dv_ref, far_ref, bar_t, d_norm_one = take(7)
+    c_send, c_got, c_half, c_half_got, bar_send, bar_got, d_send, d_got = take(8)
     sums = {}
     for name in plan.sums:
         grad, *got = take(1 + len(plan.sums[name][1]))
         sums[name] = (grad, got)
-    vec_bufs, vec_got = take(2)
+    vec_bufs, vec_got, vec_own, vec_own_got = take(4)
     send_a, recv_a, send_r, recv_r, send_s, recv_s, here = take(7)
     assert not refs
 
@@ -286,6 +331,9 @@
     for device in peers:
         pl.semaphore_signal(barrier, inc=1, device_id=device, device_id_type=MESH)
 
+    small = [pltpu.make_async_copy(a, b, here.at[10 + i]) for i, (a, b) in enumerate(zip(lines_in, lines))]
+    for copy in small:
+        copy.start()
     loads = [pltpu.make_async_copy(a, b, here.at[i]) for i, (a, b) in enumerate(zip(weights_in, weights))]
     for i in (1, 2, 0, 3, 4, 5):
         loads[i].start()
@@ -312,7 +360,7 @@
 
     def exchange(number, source, target):
         copies = []
-        for k in range(1, rows):
+        for k in sorted(range(1, rows), key=lambda k: -(k % head)):
             other, device = group_peer(k)
             copy = pltpu.make_async_remote_copy(
                 src_ref=source.at[other],
@@ -353,6 +401,8 @@
                 ref[p, a, :half, :] = jnp.where(low, part, zero)
                 ref[p, a, half:, :] = jnp.where(low, zero, part)
 
+    for copy in small:
+        copy.wait()
     own[0].wait()
     for copy in x_copies:
         copy.wait_recv()
@@ -385,16 +435,15 @@
     level = dot(pair_mean(level.shape[0]), level).astype(BF)
     c_send[0] = level[:, :width]
     c_send[1] = level[:, width:]
-    i_a = lax.broadcasted_iota(jnp.int32, (BLOCK, tokens), 0)
-    i_b = lax.broadcasted_iota(jnp.int32, (BLOCK, tokens), 1)
-    mean_all = jnp.where((i_b >> plan.local) == i_a, 0.5**plan.local, 0.0).astype(BF)
-    c_send[2] = dot(mean_all, normed).astype(BF)
+    level = dot(pair_mean(level.shape[0]), level).astype(BF)
+    c_half[: BLOCK // 2, :] = level[:, :width]
+    c_half[BLOCK // 2 :, :] = level[:, width:]
     c_copies = []
     for k in range(1, plan.groups):
         other, device = row_peer(k)
         copy = pltpu.make_async_remote_copy(
-            src_ref=c_send,
-            dst_ref=c_got.at[g],
+            src_ref=c_send if k == 1 else c_half,
+            dst_ref=c_got if k == 1 else c_half_got.at[g],
             send_sem=send_r.at[0, k],
             recv_sem=recv_r.at[0, k],
             device_id=device,
@@ -416,22 +465,33 @@
             pn[p, a, :local, :] = raised
             stats[p, a, 0:1, :] = top
             stats[p, a, 1:2, :] = jnp.sum(raised, axis=0, keepdims=True)
+            kn_t[p, a, :, :local] = turned(kn[p, a, :local, :])
+            vn_t[p, a, :, :local] = turned(vn[p, a, :local, :])
         return carry
 
-    lax.fori_loop(0, plan.pairs, attend_near, 0)
+    for p in range(plan.pairs):
+        attend_near(p, 0)
 
     for copy in c_copies:
         copy.wait_recv()
-    for index in range(3):
-        for b in range(plan.remote):
-            upper = idiv(g, 1 << b)
-            base = (upper + 1 - 2 * irem(upper, 2)) * (1 << b)
-            level = c_got[pl.ds(base, 1 << b), index].reshape(BLOCK << b, width)
-            for _ in range(b):
-                level = dot(pair_mean(level.shape[0]), level).astype(BF)
-            if index == 2:
-                bar_t[:, b * BLOCK : (b + 1) * BLOCK] = turned(level)
-                continue
+
+    def sibling(b):
+        upper = idiv(g, 1 << b)
+        return (upper + 1 - 2 * irem(upper, 2)) * (1 << b)
+
+    for b in range(plan.remote):
+        for index in range(2):
+            if b == 0:
+                level = c_got[index]
+            else:
+                count = 1 << b
+                both_kinds = c_half_got[pl.ds(sibling(b), count)].reshape(BLOCK * count, width)
+                i_r = lax.broadcasted_iota(jnp.int32, (BLOCK * count // 2, BLOCK * count), 0)
+                i_s = lax.broadcasted_iota(jnp.int32, (BLOCK * count // 2, BLOCK * count), 1)
+                own_rows = (i_r >> 3) * BLOCK + index * (BLOCK // 2) + (i_r & 7) == i_s
+                level = dot(jnp.where(own_rows, 1.0, 0.0).astype(BF), both_kinds).astype(BF)
+                for _ in range(b - 1):
+                    level = dot(pair_mean(level.shape[0]), level).astype(BF)
             for p in range(plan.pairs):
                 part = level[:, p * PAIR : (p + 1) * PAIR]
                 if b == 0:
@@ -444,8 +504,8 @@
         kr_t[p] = turned(kr[p])
         vr_t[p] = turned(vr[p])
         for a in range(2):
-            kn_t[p, a] = turned(kn[p, a])
-            vn_t[p, a] = turned(vn[p, a])
+            kn_t[p, a, :, local:] = turned(kn[p, a, local:, :])
+            vn_t[p, a, :, local:] = turned(vn[p, a, local:, :])
             q = qs[p, a]
             top_near = stats[p, a, 0:1, :]
             first_far = dot_t(kn[p, a, local:, :], q)
@@ -474,7 +534,8 @@
             mixed_t[p, DH:, a * half : (a + 1) * half] = mixed[DH:, half:].astype(BF)
         return carry
 
-    lax.fori_loop(0, plan.pairs, attend, 0)
+    for p in range(plan.pairs):
+        attend(p, 0)
 
     loads[3].wait()
     res = xg[...].reshape(tokens, width).astype(F32) + t_dot(mixed_t[...].reshape(width, tokens), wo[...])
@@ -484,78 +545,190 @@
     rs_two[...] = scale
     norm_two_b[...] = (n * gain_two[...] + shift_two[...]).astype(BF)
 
-    sums = {
+    row = lambda a: jnp.sum(a, axis=0, keepdims=True)
+    per = plan.hidden // width
+
+    def put_block(name, block, first_row, first_col):
+        r, w = plan.blocks[name]
+        row_step, col_step = min(r, block.shape[0]), min(w, block.shape[1])
+        for a in range(0, block.shape[0], row_step):
+            for b in range(0, block.shape[1], col_step):
+                s_at, h_at = (first_row + a) // r, (first_col + b) // w
+                piece = block[a : a + row_step, b : b + col_step]
+                for item in items.values():
+                    if item is not vec_sum:
+                        item.put(name, s_at, h_at, piece, (first_row + a) % r, (first_col + b) % w)
+
+    class Vectors:
+        def __init__(self):
+            self.stage, self.started = 0, []
+
+        def copy(self, source, target, slot, device):
+            copy = pltpu.make_async_remote_copy(
+                src_ref=source,
+                dst_ref=target,
+                send_sem=send_s.at[len(plan.sums), slot],
+                recv_sem=recv_s.at[len(plan.sums), slot],
+                device_id=device,
+                device_id_type=MESH,
+            )
+            copy.start()
+            self.started.append(copy)
+
+        def step(self):
+            n, k = plan.seq_bits, self.stage
+            if 0 < k <= n:
+                self.started[k - 1].wait_recv()
+                vec_bufs[k] = vec_bufs[k - 1] + vec_got[k - 1]
+            if k < n:
+                self.copy(vec_bufs.at[k], vec_got.at[k], k, (flip(s, 1 << k), h))
+            elif k == n:
+                vec = vec_bufs[n]
+                part = own_part(vec[:8])
+                vec_own[:, : part.shape[1]] = part
+                part = own_part(jnp.concatenate([vec[5 + i : 6 + i] for i in range(per)], axis=1))
+                vec_own[5:6, : part.shape[1]] = part
+                for i in range(1, head):
+                    self.copy(vec_own, vec_own_got.at[i - 1], n + i - 1, (s, flip(h, i)))
+            else:
+                values = [vec_own[...]]
+                for i in range(1, head):
+                    self.started[n + i - 1].wait_recv()
+                    values.append(vec_own_got[i - 1])
+                while len(values) > 1:
+                    values = [values[i] + values[i + 1] for i in range(0, len(values), 2)]
+                for i, line in enumerate(lines_out):
+                    line[...] = values[0][i, : line.shape[0]]
+            self.stage += 1
+
+        @property
+        def done(self):
+            return self.stage > plan.seq_bits + 1
+
+        def drain(self):
+            for copy in self.started:
+                copy.wait_send()
+
+    def own_part(line):
+        share = line.shape[1] // seq
+        part = line[:, :share]
+        for other in range(1, seq):
+            part = jnp.where(s == other, line[:, other * share : (other + 1) * share], part)
+        return part
+
+    vec_sum = Vectors()
+    items = {
         name: Summed(plan, (s, h), name, i, grad, got, send_s, recv_s, grads_out)
         for i, (name, (grad, got)) in enumerate(sums.items())
     }
-    row = lambda a: jnp.sum(a, axis=0, keepdims=True)
-
-    def step(*names):
-        for name in names:
-            if name in sums:
-                sums[name].step()
-
-    def put_all(name, block, first_row, first_col):
-        r, w = plan.blocks[name]
-        for a in range(0, block.shape[0], r):
-            for b in range(0, block.shape[1], w):
-                for item in sums.values():
-                    item.put(name, (first_row + a) // r, (first_col + b) // w, block[a : a + r, b : b + w])
-
-    loads[4].wait()
-    loads[5].wait()
-    own[1].wait()
-    for copy in dy_copies:
-        copy.wait_recv()
-    chunk = 512
-    dy = dyg[...].reshape(tokens, width)
-    for f in range(0, plan.hidden, chunk):
-        hid = dot(norm_two_b[...], wu[:, f : f + chunk]) + up_bias[:, f : f + chunk]
-        cdf = 0.5 * (1.0 + lax.erf(hid * (0.5**0.5)))
-        act = (hid * cdf).astype(BF)
-        act_ref[:, f : f + chunk] = act
-        slope_ref[:, f : f + chunk] = cdf + hid * (jnp.exp(-0.5 * hid * hid) * 0.3989422804014327)
-        put_all("down", t_dot(act, dy), f, 0)
-    step("down_a", "down_b")
-
-    hidden_rows = []
-    for i, f in enumerate(range(0, plan.hidden, chunk)):
-        dh = (dot_t(dy, wd[f : f + chunk, :]) * slope_ref[:, f : f + chunk]).astype(BF)
-        dh_ref[:, f : f + chunk] = dh
-        hidden_rows.append(row(dh.astype(F32)))
-        put_all("up", t_dot(norm_two_b[...], dh), 0, f)
-        if i == 2:
-            step("down_a", "down_b")
-    step("up_a", "up_b")
-
-    d_norm_two = dot_t(dh_ref[...], wu[...])
-    n = n_two[...]
-    dy_f = dy.astype(F32)
-    vec_bufs[0, 2:3, :] = row(d_norm_two * n)
-    vec_bufs[0, 3:4, :] = row(d_norm_two)
-    vec_bufs[0, 4:5, :] = row(dy_f)
-    per = plan.hidden // width
-    flat = jnp.concatenate(hidden_rows, axis=1)
-    for i in range(per):
-        vec_bufs[0, 5 + i : 6 + i, :] = flat[:, i * width : (i + 1) * width]
-    d_res = dy_f + norm_back(d_norm_two, n, rs_two[...], gain_two[...])
-    d_residual[...] = d_res
-    d_mix = d_res.astype(BF)
-    step("up_a", "up_b")
-    put_all("out", dot(mixed_t[...].reshape(width, tokens), d_mix), 0, 0)
-    step("out")
-    stack_heads(dos, dot_t(d_mix, wo[...]).astype(BF))
-
-    i_t = lax.broadcasted_iota(jnp.int32, (half, half), 0)
-    i_c = lax.broadcasted_iota(jnp.int32, (half, half), 1)
-    spread = jnp.zeros((half, half), F32)
-    first = 0
-    for level in range(1, plan.local):
-        spread = spread + jnp.where((i_t >> level) == (i_c - first), 0.5**level, 0.0)
-        first += half >> level
-    spread = jnp.where(i_c < first, spread, 0.0).astype(BF)
-
-    def attend_back(p, carry):
+    items["vec"] = vec_sum
+
+    def cotangent():
+        return dyg[...].reshape(tokens, width)
+
+    def blocks_of(chunk):
+        at, blocks = 0, []
+        for start, length in plan.chunks[chunk]:
+            for f in range(start, start + length, 512):
+                n = min(512, start + length - f)
+                if not blocks or blocks[-1][1] + n > 512:
+                    blocks.append([[], 0, at])
+                blocks[-1][0].append((f, n))
+                blocks[-1][1] += n
+                at += n
+        return [(segments, slice(first, first + n)) for segments, n, first in blocks]
+
+    def columns_of(ref, segments):
+        return jnp.concatenate([ref[:, f : f + n] for f, n in segments], axis=1)
+
+    def rows_of(ref, segments):
+        return jnp.concatenate([ref[f : f + n, :] for f, n in segments], axis=0)
+
+    def activate(chunk):
+        if chunk == 0:
+            loads[4].wait()
+            loads[5].wait()
+            own[1].wait()
+            for copy in dy_copies:
+                copy.wait_recv()
+        for segments, at in blocks_of(chunk):
+            hid = dot(norm_two_b[...], columns_of(wu, segments)) + columns_of(up_bias, segments)
+            cdf = 0.5 * (1.0 + lax.erf(hid * (0.5**0.5)))
+            act = (hid * cdf).astype(BF)
+            act_ref[chunk, :, at] = act
+            hid_ref[chunk, :, at] = hid
+            cdf_ref[chunk, :, at] = cdf
+            grad = t_dot(act, cotangent())
+            first = 0
+            for f, n in segments:
+                put_block("down", grad[first : first + n], f, 0)
+                first += n
+
+    def deactivate(chunk):
+        for segments, at in blocks_of(chunk):
+            hid = hid_ref[chunk, :, at]
+            slope = cdf_ref[chunk, :, at] + hid * (jnp.exp(-0.5 * hid * hid) * 0.3989422804014327)
+            dh = (dot_t(cotangent(), rows_of(wd, segments)) * slope).astype(BF)
+            dh_ref[chunk, :, at] = dh
+            sums_dh = row(dh.astype(F32))
+            grad = t_dot(norm_two_b[...], dh)
+            first = 0
+            for f, n in segments:
+                for o in range(0, n, min(n, width)):
+                    line, lane_at = divmod(f + o, width)
+                    m = min(n, width)
+                    vec_bufs[0, 5 + line : 6 + line, lane_at : lane_at + m] = sums_dh[:, first + o : first + o + m]
+                put_block("up", grad[:, first : first + n], 0, f)
+                first += n
+
+    def both(ref, weight, product, pick):
+        total = None
+        for chunk in range(2):
+            for segments, at in blocks_of(chunk):
+                term = product(ref[chunk, :, at], pick(weight, segments))
+                total = term if total is None else total + term
+        return total
+
+    def second_norm_back():
+        d_norm_two = both(dh_ref, wu, dot_t, columns_of)
+        n = n_two[...]
+        dy_f = cotangent().astype(F32)
+        vec_bufs[0, 2:3, :] = row(d_norm_two * n)
+        vec_bufs[0, 3:4, :] = row(d_norm_two)
+        vec_bufs[0, 4:5, :] = row(dy_f)
+        d_residual[...] = dy_f + norm_back(d_norm_two, n, rs_two[...], gain_two[...])
+
+    def out_grad():
+        put_block("out", dot(mixed_t[...].reshape(width, tokens), d_residual[...].astype(BF)), 0, 0)
+
+    def mixed_back():
+        stack_heads(dos, dot_t(d_residual[...].astype(BF), wo[...]).astype(BF))
+
+    def layer_output():
+        result = residual[...] + both(act_ref, wd, dot, rows_of) + down_bias[...]
+        log[...] = result.astype(BF).reshape(rows, plan.pos, width)
+
+    late_copies, own_late = [], []
+
+    def send_layer_output():
+        late_copies.extend(exchange(2, log, lo_out))
+        own_late.append(pltpu.make_async_copy(log.at[j], lo_out.at[j], here.at[8]))
+        own_late[-1].start()
+
+    spread_to = half + sum(half >> level for level in range(1, plan.local))
+
+    def spread_matrix():
+        i_t = lax.broadcasted_iota(jnp.int32, (half, half), 0)
+        i_c = lax.broadcasted_iota(jnp.int32, (half, half), 1)
+        spread = jnp.zeros((half, half), F32)
+        first = 0
+        for level in range(1, plan.local):
+            spread = spread + jnp.where((i_t >> level) == (i_c - first), 0.5**level, 0.0)
+            first += half >> level
+        return jnp.where(i_c < first, spread, 0.0).astype(BF)
+
+    def attend_back(p):
+        spread = spread_matrix()
         dk, dv, dk_far, dv_far = [], [], 0.0, 0.0
         for a in range(2):
             q, do = qs[p, a], dos[p, a]
@@ -572,7 +745,7 @@
             dq = (dot(kn_t[p, a], d_scores) + dot(kr_t[p], d_scores_far)) * (DH**-0.5)
             dq_t[p, :DH, a * half : (a + 1) * half] = dq[:DH, :half].astype(BF)
             dq_t[p, DH:, a * half : (a + 1) * half] = dq[DH:, half:].astype(BF)
-        other = half + first - BLOCK
+        other = spread_to - BLOCK
         for index, (total, total_far, ref) in enumerate(((dk, dk_far, dk_ref), (dv, dv_far, dv_ref))):
             for a in range(2):
                 coarse = jnp.concatenate(
@@ -581,151 +754,150 @@
                 ref[p, a * half : (a + 1) * half, :] = total[a][:half] + two_part_dot(spread, coarse)
             far_ref[index, p, :BLOCK, :] = total[0][local:] + total[1][local:]
             far_ref[index, p, BLOCK:, :] = total_far
-        return carry
-
-    lax.fori_loop(0, plan.pairs // 2, attend_back, 0)
-
-    result = residual[...] + dot(act_ref[...], wd[...]) + down_bias[...]
-    log[...] = result.astype(BF).reshape(rows, plan.pos, width)
-    lo_copies = exchange(2, log, lo_out)
-    lo_own = pltpu.make_async_copy(log.at[j], lo_out.at[j], here.at[8])
-    lo_own.start()
-    step("out")
-
-    lax.fori_loop(plan.pairs // 2, plan.pairs, attend_back, 0)
-
-    i_a = lax.broadcasted_iota(jnp.int32, (BLOCK, BLOCK), 0)
-    i_b = lax.broadcasted_iota(jnp.int32, (BLOCK, BLOCK), 1)
+
     d_copies = []
-    for k in range(1, plan.groups):
-        other, device = row_peer(k)
-        b = k.bit_length() - 1
-        offset = irem(other, 1 << b)
-        pick = jnp.where(((offset * BLOCK + i_a) >> b) == i_b, 0.5**b, 0.0).astype(BF)
-        for index in range(2):
-            for p in range(plan.pairs):
-                level = far_ref[index, p, BLOCK * b : BLOCK * (b + 1), :].astype(BF)
-                d_send[k, index, p] = dot(pick, level).astype(BF)
-        copy = pltpu.make_async_remote_copy(
-            src_ref=d_send.at[k],
-            dst_ref=d_got.at[k],
-            send_sem=send_r.at[1, k],
-            recv_sem=recv_r.at[1, k],
-            device_id=device,
-            device_id_type=MESH,
-        )
-        copy.start()
-        d_copies.append(copy)
-
-    d_query_t = dq_t[...].reshape(width, tokens)
-    put_all("query", dot_t(norm_t[...], d_query_t), 0, 0)
-    for index, (ref, name) in enumerate(((dk_ref, "key"), (dv_ref, "value"))):
-        mine = jnp.concatenate([ref[p].astype(BF) for p in range(plan.pairs)], axis=1)
-        made = jnp.concatenate([far_ref[index, p].astype(BF) for p in range(plan.pairs)], axis=1)
-        put_all(name, dot(norm_t[...], mine) + dot(bar_t[...], made), 0, 0)
-        if name == "key":
-            step("part_a")
-    step("part_b")
-    step("down_a", "down_b")
-    d_normed = dot_t(turned(d_query_t), wq[...])
-    step("part_a", "part_b", "out")
-
-    for copy in d_copies:
-        copy.wait_recv()
-    i_t = lax.broadcasted_iota(jnp.int32, (tokens, BLOCK), 0)
-    i_c = lax.broadcasted_iota(jnp.int32, (tokens, BLOCK), 1)
-    last = jnp.where((i_t >> plan.local) == i_c, 0.5**plan.local, 0.0).astype(BF)
-    for index, (ref, w) in enumerate(((dk_ref, wk), (dv_ref, wv))):
-        pieces = []
-        for p in range(plan.pairs):
-            coarse = d_got[1, index, p].astype(F32)
-            for k in range(2, plan.groups):
-                coarse = coarse + d_got[k, index, p].astype(F32)
-            pieces.append((ref[p] + two_part_dot(last, coarse)).astype(BF))
-        d_normed = d_normed + dot_t(jnp.concatenate(pieces, axis=1), w[...])
-    n = n_one[...]
-    vec_bufs[0, 0:1, :] = row(d_normed * n)
-    vec_bufs[0, 1:2, :] = row(d_normed)
-    vec_bufs[0, 5 + per :, :] = jnp.zeros((VEC_ROWS - 5 - per, width), F32)
-    d_first = norm_back(d_normed, n, rs_one[...], gain_one[...])
-    igg[...] = (d_residual[...] + d_first).astype(BF).reshape(rows, plan.pos, width)
-
-    vec_copies = []
-
-    def vec_start(stage):
-        if stage < plan.seq_bits:
-            jobs = [(stage, (flip(s, 1 << stage), h))]
-        else:
-            jobs = [(plan.seq_bits + k - 1, (s, flip(h, k))) for k in range(1, head)]
-        for slot, device in jobs:
+
+    def send_far():
+        i_a = lax.broadcasted_iota(jnp.int32, (BLOCK, BLOCK), 0)
+        i_b = lax.broadcasted_iota(jnp.int32, (BLOCK, BLOCK), 1)
+        for k in range(1, plan.groups):
+            other, device = row_peer(k)
+            b = k.bit_length() - 1
+            offset = irem(other, 1 << b)
+            pick = jnp.where(((offset * BLOCK + i_a) >> b) == i_b, 0.5**b, 0.0).astype(BF)
+            for index in range(2):
+                for p in range(plan.pairs):
+                    level = far_ref[index, p, BLOCK * b : BLOCK * (b + 1), :].astype(BF)
+                    d_send[k, index, p] = dot(pick, level).astype(BF)
             copy = pltpu.make_async_remote_copy(
-                src_ref=vec_bufs.at[stage],
-                dst_ref=vec_got.at[slot],
-                send_sem=send_s.at[len(plan.sums), slot],
-                recv_sem=recv_s.at[len(plan.sums), slot],
+                src_ref=d_send.at[k],
+                dst_ref=d_got.at[k],
+                send_sem=send_r.at[1, k],
+                recv_sem=recv_r.at[1, k],
                 device_id=device,
                 device_id_type=MESH,
             )
             copy.start()
-            vec_copies.append(copy)
-
-    def vec_finish(stage):
-        vec_copies[stage].wait_recv()
-        vec_bufs[stage + 1] = vec_bufs[stage] + vec_got[stage]
-
-    vec_start(0)
-    ig_copies = exchange(3, igg, ig_out)
-    ig_own = pltpu.make_async_copy(igg.at[j], ig_out.at[j], here.at[9])
-    ig_own.start()
-
-    stage = 0
-    while stage < plan.seq_bits or not all(item.done for item in sums.values()):
-        for name in ("up_a", "up_b", "down_a", "down_b", "part_a", "part_b", "out"):
-            if name in sums and not sums[name].done:
-                sums[name].step()
-        if stage < plan.seq_bits:
-            vec_finish(stage)
-            vec_start(stage + 1)
-        stage += 1
-    values = [vec_bufs[plan.seq_bits]]
-    for k in range(1, head):
-        vec_copies[plan.seq_bits + k - 1].wait_recv()
-        values.append(vec_got[plan.seq_bits + k - 1])
-    while len(values) > 1:
-        values = [values[i] + values[i + 1] for i in range(0, len(values), 2)]
-    vec = values[0]
-
-    def own_part(line):
-        share = line.shape[1] // seq
-        part = line[:, :share]
-        for other in range(1, seq):
-            part = jnp.where(s == other, line[:, other * share : (other + 1) * share], part)
-        return part
-
-    vec_out[...] = jnp.zeros_like(vec_out)
-    part = own_part(vec[:8])
-    vec_out[:, : part.shape[1]] = part
-    part = own_part(jnp.concatenate([vec[5 + i : 6 + i] for i in range(per)], axis=1))
-    vec_out[5:6, : part.shape[1]] = part
-
-    for copy in lo_copies + ig_copies:
+            d_copies.append(copy)
+
+    def part_grads():
+        put_block("query", dot_t(norm_t[...], dq_t[...].reshape(width, tokens)), 0, 0)
+        for index, (ref, name) in enumerate(((dk_ref, "key"), (dv_ref, "value"))):
+            mine = jnp.concatenate([ref[p].astype(BF) for p in range(plan.pairs)], axis=1)
+            made = jnp.concatenate([far_ref[index, p].astype(BF) for p in range(plan.pairs)], axis=1)
+            put_block(name, dot(norm_t[...], mine) + dot(bar_t[...], made), 0, 0)
+
+    bar_copies = []
+
+    def send_bars():
+        i_a = lax.broadcasted_iota(jnp.int32, (BLOCK, tokens), 0)
+        i_b = lax.broadcasted_iota(jnp.int32, (BLOCK, tokens), 1)
+        mean_all = jnp.where((i_b >> plan.local) == i_a, 0.5**plan.local, 0.0).astype(BF)
+        bar_send[...] = dot_t(mean_all, norm_t[...]).astype(BF)
+        for k in range(1, plan.groups):
+            other, device = row_peer(k)
+            copy = pltpu.make_async_remote_copy(
+                src_ref=bar_send,
+                dst_ref=bar_got.at[g],
+                send_sem=send_r.at[2, k],
+                recv_sem=recv_r.at[2, k],
+                device_id=device,
+                device_id_type=MESH,
+            )
+            copy.start()
+            bar_copies.append(copy)
+
+    def take_bars():
+        for copy in bar_copies:
+            copy.wait_recv()
+        for b in range(plan.remote):
+            level = bar_got[pl.ds(sibling(b), 1 << b)].reshape(BLOCK << b, width)
+            for _ in range(b):
+                level = dot(pair_mean(level.shape[0]), level).astype(BF)
+            bar_t[:, b * BLOCK : (b + 1) * BLOCK] = turned(level)
+
+    def query_back():
+        d_norm_one[...] = dot_t(turned(dq_t[...].reshape(width, tokens)), wq[...])
+
+    def take_far():
+        for copy in d_copies:
+            copy.wait_recv()
+
+    def first_norm_back():
+        i_t = lax.broadcasted_iota(jnp.int32, (tokens, BLOCK), 0)
+        i_c = lax.broadcasted_iota(jnp.int32, (tokens, BLOCK), 1)
+        last = jnp.where((i_t >> plan.local) == i_c, 0.5**plan.local, 0.0).astype(BF)
+        d_normed = d_norm_one[...]
+        for index, (ref, w) in enumerate(((dk_ref, wk), (dv_ref, wv))):
+            pieces = []
+            for p in range(plan.pairs):
+                coarse = d_got[1, index, p].astype(F32)
+                for k in range(2, plan.groups):
+                    coarse = coarse + d_got[k, index, p].astype(F32)
+                pieces.append((ref[p] + two_part_dot(last, coarse)).astype(BF))
+            d_normed = d_normed + dot_t(jnp.concatenate(pieces, axis=1), w[...])
+        n = n_one[...]
+        vec_bufs[0, 0:1, :] = row(d_normed * n)
+        vec_bufs[0, 1:2, :] = row(d_normed)
+        vec_bufs[0, 5 + per :, :] = jnp.zeros((VEC_ROWS - 5 - per, width), F32)
+        d_first = norm_back(d_normed, n, rs_one[...], gain_one[...])
+        igg[...] = (d_residual[...] + d_first).astype(BF).reshape(rows, plan.pos, width)
+
+    def send_input_grad():
+        late_copies.extend(exchange(3, igg, ig_out))
+        own_late.append(pltpu.make_async_copy(igg.at[j], ig_out.at[j], here.at[9]))
+        own_late[-1].start()
+
+    vec_own[...] = jnp.zeros_like(vec_own)
+    work = {
+        "ffn1a": lambda: activate(0),
+        "ffn1b": lambda: activate(1),
+        "ffn2a": lambda: deactivate(0),
+        "ffn2b": lambda: deactivate(1),
+        "ln2b": second_norm_back,
+        "outg": out_grad,
+        "lo": layer_output,
+        "Alo": send_layer_output,
+        "dmix": mixed_back,
+        "Abar": send_bars,
+        "bar": take_bars,
+        "dsend": send_far,
+        "qkvg": part_grads,
+        "dnq": query_back,
+        "Wd": take_far,
+        "ln1b": first_norm_back,
+        "Aig": send_input_grad,
+    }
+    first_pairs = {f"ab{i}": range(i, plan.pairs, 4) for i in range(4)}
+    for name in ORDER:
+        if name in work:
+            work[name]()
+        elif name in first_pairs:
+            for p in first_pairs[name]:
+                attend_back(p)
+        elif name in items:
+            items[name].step()
+    while not all(item.done for item in items.values()):
+        for item in items.values():
+            if not item.done:
+                item.step()
+
+    for copy in late_copies:
         copy.wait_recv()
-    lo_own.wait()
-    ig_own.wait()
-    for copy in x_copies + dy_copies + lo_copies + ig_copies + c_copies + d_copies + vec_copies:
+    for copy in own_late:
+        copy.wait()
+    for copy in x_copies + dy_copies + c_copies + bar_copies + d_copies + late_copies:
         copy.wait_send()
-    for item in sums.values():
+    for item in items.values():
         item.drain()
 
 
 def place_kernel(*refs):
-    ins, outs, sems = refs[:9], refs[9:-1], refs[-1]
-    vec, lines = ins[-1], outs[8:]
-    copies = [pltpu.make_async_copy(ins[i], outs[i], sems.at[i]) for i in range(8)]
+    count = len(refs) // 2
+    ins, outs, sems = refs[:count], refs[count:-1], refs[-1]
+    copies = [pltpu.make_async_copy(a, b, sems.at[i]) for i, (a, b) in enumerate(zip(ins, outs))]
     for copy in copies:
         copy.start()
-    for i, line in enumerate(lines):
-        line[...] = vec[i, : line.shape[0]]
     for copy in copies:
         copy.wait()
 
@@ -759,6 +931,7 @@
 
     scratch = [buf(rows, pos, width)] * 4
     scratch += [buf(width, width)] * 4 + [buf(width, hidden), buf(hidden, width)]
+    scratch += [buf(1, n, dtype=F32) for n in (width, width, width, width, hidden, width)]
     scratch += [
         buf(width, tokens),
         buf(tokens, width, dtype=F32),
@@ -787,7 +960,8 @@
         buf(near, tokens, dtype=F32),
         buf(pairs, PAIR, tokens),
     ]
-    scratch += [buf(tokens, hidden), buf(tokens, hidden, dtype=F32), buf(tokens, hidden)]
+    part = sum(n for _, n in plan.chunks[0])
+    scratch += [buf(2, tokens, part)] + [buf(2, tokens, part, dtype=F32)] * 2 + [buf(2, tokens, part)]
     scratch += [
         buf(pairs, 2, tokens, PAIR),
         buf(pairs, PAIR, tokens),
@@ -795,10 +969,15 @@
         buf(pairs, tokens, PAIR, dtype=F32),
         buf(2, pairs, BLOCK * plan.remote, PAIR, dtype=F32),
         buf(width, BLOCK * plan.remote),
+        buf(tokens, width, dtype=F32),
     ]
     scratch += [
-        buf(3, BLOCK, width),
-        buf(groups, 3, BLOCK, width),
+        buf(2, BLOCK, width),
+        buf(2, BLOCK, width),
+        buf(BLOCK, width),
+        buf(groups, BLOCK, width),
+        buf(BLOCK, width),
+        buf(groups, BLOCK, width),
         buf(groups, 2, pairs, BLOCK, PAIR),
         buf(groups, 2, pairs, BLOCK, PAIR),
     ]
@@ -806,22 +985,25 @@
         scratch += [buf(*(2,) * plan.bits, *plan.sum_shape(name))]
         scratch += [buf(*shape) for shape in plan.got_shapes(name)]
     slots = plan.bits + plan.head
+    share = max(width, hidden) // plan.seq
     scratch += [
         buf(plan.seq_bits + 1, VEC_ROWS, width, dtype=F32),
-        buf(plan.seq_bits + plan.head - 1, VEC_ROWS, width, dtype=F32),
+        buf(plan.seq_bits, VEC_ROWS, width, dtype=F32),
+        buf(8, share, dtype=F32),
+        buf(plan.head - 1, 8, share, dtype=F32),
     ]
     dma = pltpu.SemaphoreType.DMA
-    scratch += [dma((4, rows)), dma((4, rows)), dma((2, groups)), dma((2, groups))]
-    scratch += [dma((len(plan.sums) + 1, slots)), dma((len(plan.sums) + 1, slots)), dma((10,))]
+    scratch += [dma((4, rows)), dma((4, rows)), dma((3, groups)), dma((3, groups))]
+    scratch += [dma((len(plan.sums) + 1, slots)), dma((len(plan.sums) + 1, slots)), dma((16,))]
 
     line = lambda a: a.reshape(1, -1)
     big = [jax.ShapeDtypeStruct(inputs.shape, BF)] * 2 + [jax.ShapeDtypeStruct(plan.blocks[n], F32) for n in names]
-    share = max(width, hidden) // plan.seq
+    lines = [jax.ShapeDtypeStruct((width // plan.seq,), F32)] * 5 + [jax.ShapeDtypeStruct((hidden // plan.seq,), F32)]
     results = pl.pallas_call(
         functools.partial(layer_kernel, plan),
-        out_shape=big + [jax.ShapeDtypeStruct((8, share), F32)],
-        in_specs=[anywhere, anywhere] + [vmem] * 6 + [anywhere] * 6,
-        out_specs=[anywhere, anywhere] + [vmem] * 7,
+        out_shape=[pltpu.VMEM(o.shape, o.dtype) for o in big + lines],
+        in_specs=[anywhere] * 14,
+        out_specs=[vmem] * 14,
         scratch_shapes=scratch,
         compiler_params=pltpu.CompilerParams(
             collective_id=0, has_side_effects=True, vmem_limit_bytes=56 << 20
@@ -843,15 +1025,14 @@
         up_weight,
         down_weight,
     )
-    lines = [jax.ShapeDtypeStruct((width // plan.seq,), F32)] * 5 + [jax.ShapeDtypeStruct((hidden // plan.seq,), F32)]
     placed = pl.pallas_call(
         place_kernel,
         out_shape=big + lines,
-        in_specs=[anywhere] * 8 + [vmem],
-        out_specs=[vmem] * 14,
-        scratch_shapes=[dma((8,))],
+        in_specs=[vmem] * 14,
+        out_specs=[anywhere] * 14,
+        scratch_shapes=[dma((14,))],
         name="place",
-    )(*results)
+    )(*[pltpu.with_memory_space_constraint(r, pltpu.VMEM) for r in results])
     layer_out, input_grad, down_g, up_g, out_g, query_g, key_g, value_g = placed[:8]
     gain_one_g, shift_one_g, gain_two_g, shift_two_g, down_bias_g, up_bias_g = placed[8:]
     return (

time: 75 us -> 64.9 us (0.87)
  Pallas kernels: 74.1 us -> 63.9 us
    pallas_call x2, Pallas kernels: 74.1 us -> 63.9 us  [the longest x1 62.8 us: body(): pl.pallas_call(functools.partial(layer_kernel, plan), out_shape=[pltpu.VM...]
where the time goes in v3:
time: 64.9 us; the launch traced here: 64.7 us
  Pallas kernels  63.9 us (98%)
  between operations  0.82 us (1%)
    pallas_call x1, Pallas kernels, body(): pl.pallas_call(functools.partial(layer_kernel, plan), out_shape=[pltpu.VM...  62.8 us

profile of v3, /device:TPU:0, one launch (start us, length us, event | category | flops | bytes accessed | tf_op | source)
XLA Modules:
  0.0 64.7 jit_solution(9075412707474523304)
XLA Ops:
  0.7 62.8 %layer.1 = (bf16[8,32,512]{2,1,0:T(8,128)(2,1)S(1)}, bf16[8,32,512]{2,1,0:T(8,128)(2,1)S(1)}, f32[256,128]{1,0:T(8,128)S(1)}, f32[64,512]{1,0:T(8,128)S(1)}, f32...) custom-call(bf16[8,32,512]{2,1,0:T(8,128)(2,1)} %refs_0_.1, ...), custom_call_target="tpu_custom_call" | custom-call | tf_op jit(solution)/shard_map/layer/pallas_call | solution.py:1002
  63.5 1.1 %place.1 = (bf16[8,32,512]{2,1,0:T(8,128)(2,1)}, bf16[8,32,512]{2,1,0:T(8,128)(2,1)}, f32[256,128]{1,0:T(8,128)}, f32[64,512]{1,0:T(8,128)}, f32[64,128]{1,0:T(8...) custom-call(bf16[8,32,512]{2,1,0:T(8,128)(2,1)S(1)} %get-tuple-eleme, ...), custom_call_target="tpu_custom_call" | custom-call | tf_op jit(solution)/shard_map/place/pallas_call | solution.py:1028

commit v4 on v3

--- a/solution.py
+++ b/solution.py
@@ -14,26 +14,26 @@
 BLOCK = 16
 EPSILON = 1e-05
 PAIR = 2 * DH
-VEC_ROWS = 16
 LANES = 128
 ORDER = (
-    "ffn1a", "dna", "ffn1b", "Abar", "dnb", "dnc", "dna", "ffn2a", "upa", "dnc", "dnb", "ffn2b", "lo", "Alo",
-    "upb", "ln2b", "outg", "upa", "dmix", "bar", "upb", "ab0", "ab1", "dnb", "dnc", "outa", "outa", "ab2",
-    "ab3", "dna", "dsend", "qkvg", "dnb", "outa", "upb", "dnq", "pa", "pb", "upa", "dnb", "pb", "dnc", "dna",
-    "Wd", "ln1b", "vec", "pa", "upb", "dnc", "upa", "Aig", "dna", "vec", "outa", "pb", "outa", "vec", "upb",
-    "dnc", "dnb", "upa", "pa", "pb", "vec", "pa", "upa", "vec", "outa", "pa", "pb", "upb",
+    "f10", "f13", "f11", "g10", "g11", "dnc", "f12", "g12", "g13", "dnb", "f21", "dnc", "Abar", "dna", "f20",
+    "dnb", "dna", "upa", "f23", "f22", "lo", "upb", "upa", "Alo", "ln2b", "dmix", "outg", "ab3", "upb",
+    "outa", "ab0", "outa", "ab2", "ab1", "dnc", "dnb", "bar", "dnq", "qkvg", "dsend", "pb", "pb", "pa", "upa",
+    "pa", "outa", "upb", "dnb", "Wd", "ln1b", "vec", "Aig", "dnb", "upa", "vec", "dna", "pb", "upb", "outa",
+    "pa", "dnc", "vec", "pb", "dna", "pa", "vec", "upa", "pb", "outa", "dna", "dnb", "dnc", "upb", "pa",
+    "dna", "dnc", "pb", "upa", "vec", "outa", "pa",
 )
 STAGES = {
-    "dna": ("straight", "head"),
+    "dna": ("straight", "bits"),
     "dnb": ("back", "bits"),
     "dnc": ("bits", "straight"),
     "upa": ("straight", "bits"),
-    "upb": ("back", "bits"),
-    "outa": ("bits", "straight"),
-    "pa": ("straight", "head"),
-    "pb": ("back", "head"),
+    "upb": ("back", "head"),
+    "outa": ("bits", "back"),
+    "pa": ("back", "bits"),
+    "pb": ("straight", "bits"),
 }
-EIGHTHS = 2
+EIGHTHS = 6
 
 
 def idiv(value, k):
@@ -108,8 +108,9 @@
         self.seq_bits = seq.bit_length() - 1
         self.head_bits = head.bit_length() - 1
         self.bits = self.seq_bits + self.head_bits
-        self.near = self.half * 2
-        self.far = BLOCK * (self.remote - 1)
+        self.near = self.half + sum(self.half >> level for level in range(1, self.local))
+        self.lines = 5 + hidden // width
+        self.far = BLOCK * self.remote
         cols = width // head
         self.blocks = {
             "down": (hidden // seq, cols),
@@ -143,11 +144,8 @@
             lanes = lambda cs: [("up", 0, rows_up, c, c + LANES) for a, b in cs for c in range(a, b, LANES)]
             self.sums = {
                 "dna": (tall("down", (0, half_down - third)), stages["dna"]),
-                "dnb": (tall("down", (half_down, half_down - third)), stages["dnb"]),
-                "dnc": (
-                    tall("down", (half_down - third, third), (2 * half_down - third, third)),
-                    stages["dnc"],
-                ),
+                "dnb": (tall("down", (half_down, half_down)), stages["dnb"]),
+                "dnc": (tall("down", (half_down - third, third)), stages["dnc"]),
                 "upa": (lanes(first), stages["upa"]),
                 "upb": (lanes(second), stages["upb"]),
             }
@@ -299,11 +297,11 @@
     wq, wk, wv, wo, wu, wd = weights = take(6)
     gain_one, shift_one, gain_two, shift_two, up_bias, down_bias = lines = take(6)
     norm_t, n_one, rs_one, n_two, rs_two, norm_two_b, residual, d_residual = take(8)
-    qs, kn, vn, kr, vr, kn_t, vn_t, kr_t, vr_t = take(9)
-    pn, pr, stats, mask, mixed_t = take(5)
+    qs, kn, vn, kf, vf, near_values = take(6)
+    pn, pf, stats, mask, mixed_t = take(5)
     act_ref, hid_ref, cdf_ref, dh_ref = take(4)
     dos, dq_t, dk_ref, dv_ref, far_ref, bar_t, d_norm_one = take(7)
-    c_send, c_got, c_half, c_half_got, bar_send, bar_got, d_send, d_got = take(8)
+    c_send, c_got, c_half, c_half_got, bar_send, bar_got, d_send, d_got, d_half, d_half_got, far_parts = take(11)
     sums = {}
     for name in plan.sums:
         grad, *got = take(1 + len(plan.sums[name][1]))
@@ -404,9 +402,12 @@
     for copy in small:
         copy.wait()
     own[0].wait()
-    for copy in x_copies:
+    near_first = x_copies[::-1]
+    for copy in near_first[:-2]:
         copy.wait_recv()
     dy_copies = exchange(1, dy_in, dyg)
+    for copy in near_first[-2:]:
+        copy.wait_recv()
     x = xg[...].reshape(tokens, width).astype(F32)
     n, scale = norm_stats(x)
     n_one[...] = n
@@ -455,22 +456,20 @@
     loads[0].wait()
     stack_heads(qs, (dot(normed, wq[...]) * (DH**-0.5)).astype(BF))
     norm_t[...] = turned(normed)
-    local = near - BLOCK
-
-    def attend_near(p, carry):
+
+    def attend_near(p):
         for a in range(2):
-            scores = dot_t(kn[p, a, :local, :], qs[p, a]) + mask[:local, :]
+            at = slice((2 * p + a) * tokens, (2 * p + a + 1) * tokens)
+            scores = dot_t(kn[p, a], qs[p, a]) + mask[...]
             top = jnp.max(scores, axis=0, keepdims=True)
             raised = jnp.exp(scores - top)
-            pn[p, a, :local, :] = raised
-            stats[p, a, 0:1, :] = top
-            stats[p, a, 1:2, :] = jnp.sum(raised, axis=0, keepdims=True)
-            kn_t[p, a, :, :local] = turned(kn[p, a, :local, :])
-            vn_t[p, a, :, :local] = turned(vn[p, a, :local, :])
-        return carry
+            pn[p, a] = raised
+            stats[0:1, at] = top
+            stats[1:2, at] = jnp.sum(raised, axis=0, keepdims=True)
+            near_values[p, a] = dot(turned(vn[p, a]), raised.astype(BF))
 
     for p in range(plan.pairs):
-        attend_near(p, 0)
+        attend_near(p)
 
     for copy in c_copies:
         copy.wait_recv()
@@ -494,48 +493,25 @@
                     level = dot(pair_mean(level.shape[0]), level).astype(BF)
             for p in range(plan.pairs):
                 part = level[:, p * PAIR : (p + 1) * PAIR]
-                if b == 0:
-                    for a in range(2):
-                        targets[index][p, a, local:, :] = part
-                else:
-                    (kr, vr)[index][p, (b - 1) * BLOCK : b * BLOCK, :] = part
-
-    def attend(p, carry):
-        kr_t[p] = turned(kr[p])
-        vr_t[p] = turned(vr[p])
-        for a in range(2):
-            kn_t[p, a, :, local:] = turned(kn[p, a, local:, :])
-            vn_t[p, a, :, local:] = turned(vn[p, a, local:, :])
-            q = qs[p, a]
-            top_near = stats[p, a, 0:1, :]
-            first_far = dot_t(kn[p, a, local:, :], q)
-            rest_far = dot_t(kr[p], q)
-            top = jnp.maximum(
-                top_near,
-                jnp.maximum(
-                    jnp.max(first_far, axis=0, keepdims=True), jnp.max(rest_far, axis=0, keepdims=True)
-                ),
-            )
-            shrink = jnp.exp(top_near - top)
-            first_far = jnp.exp(first_far - top)
-            rest_far = jnp.exp(rest_far - top)
-            total = (
-                stats[p, a, 1:2, :] * shrink
-                + jnp.sum(first_far, axis=0, keepdims=True)
-                + jnp.sum(rest_far, axis=0, keepdims=True)
-            )
-            share = 1.0 / total
-            pn[p, a, :local, :] = pn[p, a, :local, :] * (shrink * share)
-            pn[p, a, local:, :] = first_far * share
-            rest_far = rest_far * share
-            pr[p, a] = rest_far
-            mixed = dot(vn_t[p, a], pn[p, a].astype(BF)) + dot(vr_t[p], rest_far.astype(BF))
-            mixed_t[p, :DH, a * half : (a + 1) * half] = mixed[:DH, :half].astype(BF)
-            mixed_t[p, DH:, a * half : (a + 1) * half] = mixed[DH:, half:].astype(BF)
-        return carry
-
-    for p in range(plan.pairs):
-        attend(p, 0)
+                (kf, vf)[index][p, b * BLOCK : (b + 1) * BLOCK, :] = part
+
+    halves = [(p, a) for p in range(plan.pairs) for a in range(2)]
+    scores = jnp.concatenate([dot_t(kf[p], qs[p, a]) for p, a in halves], axis=1)
+    top_near = stats[0:1, :]
+    top = jnp.maximum(top_near, jnp.max(scores, axis=0, keepdims=True))
+    shrink = jnp.exp(top_near - top)
+    raised = jnp.exp(scores - top)
+    share = 1.0 / (stats[1:2, :] * shrink + jnp.sum(raised, axis=0, keepdims=True))
+    near_share = shrink * share
+    stats[2:3, :] = near_share
+    prob = raised * share
+    pf[...] = prob
+    prob = prob.astype(BF)
+    for i, (p, a) in enumerate(halves):
+        at = slice(i * tokens, (i + 1) * tokens)
+        mixed = near_values[p, a] * near_share[:, at] + t_dot(vf[p], prob[:, at])
+        mixed_t[p, :DH, a * half : (a + 1) * half] = mixed[:DH, :half].astype(BF)
+        mixed_t[p, DH:, a * half : (a + 1) * half] = mixed[DH:, half:].astype(BF)
 
     loads[3].wait()
     res = xg[...].reshape(tokens, width).astype(F32) + t_dot(mixed_t[...].reshape(width, tokens), wo[...])
@@ -644,28 +620,35 @@
     def rows_of(ref, segments):
         return jnp.concatenate([ref[f : f + n, :] for f, n in segments], axis=0)
 
-    def activate(chunk):
-        if chunk == 0:
+    flat = [(chunk, *block) for chunk in range(2) for block in blocks_of(chunk)]
+    quarters = [flat[i : i + 1] for i in range(4)] if plan.fine else [flat, [], [], []]
+
+    def activate(quarter):
+        if quarter == 0:
             loads[4].wait()
-            loads[5].wait()
-            own[1].wait()
-            for copy in dy_copies:
-                copy.wait_recv()
-        for segments, at in blocks_of(chunk):
+        for chunk, segments, at in quarters[quarter]:
             hid = dot(norm_two_b[...], columns_of(wu, segments)) + columns_of(up_bias, segments)
             cdf = 0.5 * (1.0 + lax.erf(hid * (0.5**0.5)))
             act = (hid * cdf).astype(BF)
             act_ref[chunk, :, at] = act
             hid_ref[chunk, :, at] = hid
             cdf_ref[chunk, :, at] = cdf
-            grad = t_dot(act, cotangent())
+
+    def down_grad(quarter):
+        if quarter == 0:
+            loads[5].wait()
+            own[1].wait()
+            for copy in dy_copies:
+                copy.wait_recv()
+        for chunk, segments, at in quarters[quarter]:
+            grad = t_dot(act_ref[chunk, :, at], cotangent())
             first = 0
             for f, n in segments:
                 put_block("down", grad[first : first + n], f, 0)
                 first += n
 
-    def deactivate(chunk):
-        for segments, at in blocks_of(chunk):
+    def deactivate(quarter):
+        for chunk, segments, at in quarters[quarter]:
             hid = hid_ref[chunk, :, at]
             slope = cdf_ref[chunk, :, at] + hid * (jnp.exp(-0.5 * hid * hid) * 0.3989422804014327)
             dh = (dot_t(cotangent(), rows_of(wd, segments)) * slope).astype(BF)
@@ -715,26 +698,26 @@
         own_late.append(pltpu.make_async_copy(log.at[j], lo_out.at[j], here.at[8]))
         own_late[-1].start()
 
-    spread_to = half + sum(half >> level for level in range(1, plan.local))
-
     def spread_matrix():
-        i_t = lax.broadcasted_iota(jnp.int32, (half, half), 0)
-        i_c = lax.broadcasted_iota(jnp.int32, (half, half), 1)
-        spread = jnp.zeros((half, half), F32)
+        i_t = lax.broadcasted_iota(jnp.int32, (half, near - half), 0)
+        i_c = lax.broadcasted_iota(jnp.int32, (half, near - half), 1)
+        spread = jnp.zeros((half, near - half), F32)
         first = 0
         for level in range(1, plan.local):
             spread = spread + jnp.where((i_t >> level) == (i_c - first), 0.5**level, 0.0)
             first += half >> level
-        return jnp.where(i_c < first, spread, 0.0).astype(BF)
+        return spread.astype(BF)
 
     def attend_back(p):
         spread = spread_matrix()
         dk, dv, dk_far, dv_far = [], [], 0.0, 0.0
+        k_far, v_far = kf[p], vf[p]
         for a in range(2):
+            at = slice((2 * p + a) * tokens, (2 * p + a + 1) * tokens)
             q, do = qs[p, a], dos[p, a]
-            prob, prob_far = pn[p, a], pr[p, a]
+            prob, prob_far = pn[p, a] * stats[2:3, at], pf[:, at]
             d_prob = dot_t(vn[p, a], do)
-            d_prob_far = dot_t(vr[p], do)
+            d_prob_far = dot_t(v_far, do)
             inner = row(prob * d_prob) + row(prob_far * d_prob_far)
             d_scores = (prob * (d_prob - inner)).astype(BF)
             d_scores_far = (prob_far * (d_prob_far - inner)).astype(BF)
@@ -742,18 +725,15 @@
             dv.append(dot(prob.astype(BF), do))
             dk_far = dk_far + dot(d_scores_far, q)
             dv_far = dv_far + dot(prob_far.astype(BF), do)
-            dq = (dot(kn_t[p, a], d_scores) + dot(kr_t[p], d_scores_far)) * (DH**-0.5)
+            dq = (t_dot(kn[p, a], d_scores) + t_dot(k_far, d_scores_far)) * (DH**-0.5)
             dq_t[p, :DH, a * half : (a + 1) * half] = dq[:DH, :half].astype(BF)
             dq_t[p, DH:, a * half : (a + 1) * half] = dq[DH:, half:].astype(BF)
-        other = spread_to - BLOCK
+        other = near - BLOCK
         for index, (total, total_far, ref) in enumerate(((dk, dk_far, dk_ref), (dv, dv_far, dv_ref))):
             for a in range(2):
-                coarse = jnp.concatenate(
-                    [total[a][half:other], total[1 - a][other : other + BLOCK], total[a][local:]], axis=0
-                )
+                coarse = jnp.concatenate([total[a][half:other], total[1 - a][other:]], axis=0)
                 ref[p, a * half : (a + 1) * half, :] = total[a][:half] + two_part_dot(spread, coarse)
-            far_ref[index, p, :BLOCK, :] = total[0][local:] + total[1][local:]
-            far_ref[index, p, BLOCK:, :] = total_far
+            far_ref[index, p] = total_far
 
     d_copies = []
 
@@ -764,14 +744,22 @@
             other, device = row_peer(k)
             b = k.bit_length() - 1
             offset = irem(other, 1 << b)
-            pick = jnp.where(((offset * BLOCK + i_a) >> b) == i_b, 0.5**b, 0.0).astype(BF)
             for index in range(2):
                 for p in range(plan.pairs):
                     level = far_ref[index, p, BLOCK * b : BLOCK * (b + 1), :].astype(BF)
-                    d_send[k, index, p] = dot(pick, level).astype(BF)
+                    if b == 0:
+                        d_send[index, p] = level
+                        continue
+                    rows_at = (offset * (BLOCK // 2) + (i_a & 7)) >> (b - 1)
+                    pick = jnp.where((rows_at == i_b) & ((i_a >> 3) == index), 0.5**b, 0.0).astype(BF)
+                    part = dot(pick, level)
+                    if index == 0:
+                        far_parts[p] = part
+                    else:
+                        d_half[k, p] = (far_parts[p] + part).astype(BF)
             copy = pltpu.make_async_remote_copy(
-                src_ref=d_send.at[k],
-                dst_ref=d_got.at[k],
+                src_ref=d_send if k == 1 else d_half.at[k],
+                dst_ref=d_got if k == 1 else d_half_got.at[k],
                 send_sem=send_r.at[1, k],
                 recv_sem=recv_r.at[1, k],
                 device_id=device,
@@ -827,19 +815,25 @@
         i_t = lax.broadcasted_iota(jnp.int32, (tokens, BLOCK), 0)
         i_c = lax.broadcasted_iota(jnp.int32, (tokens, BLOCK), 1)
         last = jnp.where((i_t >> plan.local) == i_c, 0.5**plan.local, 0.0).astype(BF)
+        half_of = [
+            jnp.where((i_t >> (plan.local + 1)) == i_c - (BLOCK // 2) * i, 0.5**plan.local, 0.0).astype(BF)
+            for i in range(2)
+        ]
         d_normed = d_norm_one[...]
         for index, (ref, w) in enumerate(((dk_ref, wk), (dv_ref, wv))):
             pieces = []
             for p in range(plan.pairs):
-                coarse = d_got[1, index, p].astype(F32)
-                for k in range(2, plan.groups):
-                    coarse = coarse + d_got[k, index, p].astype(F32)
-                pieces.append((ref[p] + two_part_dot(last, coarse)).astype(BF))
+                total = ref[p] + dot(last, d_got[index, p])
+                if plan.groups > 2:
+                    coarse = d_half_got[2, p].astype(F32)
+                    for k in range(3, plan.groups):
+                        coarse = coarse + d_half_got[k, p].astype(F32)
+                    total = total + two_part_dot(half_of[index], coarse)
+                pieces.append(total.astype(BF))
             d_normed = d_normed + dot_t(jnp.concatenate(pieces, axis=1), w[...])
         n = n_one[...]
         vec_bufs[0, 0:1, :] = row(d_normed * n)
         vec_bufs[0, 1:2, :] = row(d_normed)
-        vec_bufs[0, 5 + per :, :] = jnp.zeros((VEC_ROWS - 5 - per, width), F32)
         d_first = norm_back(d_normed, n, rs_one[...], gain_one[...])
         igg[...] = (d_residual[...] + d_first).astype(BF).reshape(rows, plan.pos, width)
 
@@ -850,10 +844,9 @@
 
     vec_own[...] = jnp.zeros_like(vec_own)
     work = {
-        "ffn1a": lambda: activate(0),
-        "ffn1b": lambda: activate(1),
-        "ffn2a": lambda: deactivate(0),
-        "ffn2b": lambda: deactivate(1),
+        **{f"f1{i}": functools.partial(activate, i) for i in range(4)},
+        **{f"g1{i}": functools.partial(down_grad, i) for i in range(4)},
+        **{f"f2{i}": functools.partial(deactivate, i) for i in range(4)},
         "ln2b": second_norm_back,
         "outg": out_grad,
         "lo": layer_output,
@@ -948,15 +941,12 @@
         buf(pairs, 2, near, PAIR),
         buf(pairs, far, PAIR),
         buf(pairs, far, PAIR),
-        buf(pairs, 2, PAIR, near),
-        buf(pairs, 2, PAIR, near),
-        buf(pairs, PAIR, far),
-        buf(pairs, PAIR, far),
+        buf(pairs, 2, PAIR, tokens, dtype=F32),
     ]
     scratch += [
         buf(pairs, 2, near, tokens, dtype=F32),
-        buf(pairs, 2, far, tokens, dtype=F32),
-        buf(pairs, 2, 8, tokens, dtype=F32),
+        buf(far, 2 * pairs * tokens, dtype=F32),
+        buf(8, 2 * pairs * tokens, dtype=F32),
         buf(near, tokens, dtype=F32),
         buf(pairs, PAIR, tokens),
     ]
@@ -978,8 +968,11 @@
         buf(groups, BLOCK, width),
         buf(BLOCK, width),
         buf(groups, BLOCK, width),
-        buf(groups, 2, pairs, BLOCK, PAIR),
-        buf(groups, 2, pairs, BLOCK, PAIR),
+        buf(2, pairs, BLOCK, PAIR),
+        buf(2, pairs, BLOCK, PAIR),
+        buf(groups, pairs, BLOCK, PAIR),
+        buf(groups, pairs, BLOCK, PAIR),
+        buf(pairs, BLOCK, PAIR, dtype=F32),
     ]
     for name in plan.sums:
         scratch += [buf(*(2,) * plan.bits, *plan.sum_shape(name))]
@@ -987,8 +980,8 @@
     slots = plan.bits + plan.head
     share = max(width, hidden) // plan.seq
     scratch += [
-        buf(plan.seq_bits + 1, VEC_ROWS, width, dtype=F32),
-        buf(plan.seq_bits, VEC_ROWS, width, dtype=F32),
+        buf(plan.seq_bits + 1, plan.lines, width, dtype=F32),
+        buf(plan.seq_bits, plan.lines, width, dtype=F32),
         buf(8, share, dtype=F32),
         buf(plan.head - 1, 8, share, dtype=F32),
     ]

time: 64.9 us -> 60.7 us (0.935)
  Pallas kernels: 63.9 us -> 59.7 us
    pallas_call x1, Pallas kernels: 62.8 us -> 58.7 us  [body(): pl.pallas_call(functools.partial(layer_kernel, plan), out_shape=[pltpu.VM...]
where the time goes in v4:
time: 60.7 us; the launch traced here: 60.5 us
  Pallas kernels  59.7 us (98%)
  between operations  0.82 us (1%)
    pallas_call x1, Pallas kernels, body(): pl.pallas_call(functools.partial(layer_kernel, plan), out_shape=[pltpu.VM...  58.7 us

profile of v4, /device:TPU:0, one launch (start us, length us, event | category | flops | bytes accessed | tf_op | source)
XLA Modules:
  0.0 60.5 jit_solution(10322413846666720460)
XLA Ops:
  0.7 58.7 %layer.1 = (bf16[8,32,512]{2,1,0:T(8,128)(2,1)S(1)}, bf16[8,32,512]{2,1,0:T(8,128)(2,1)S(1)}, f32[256,128]{1,0:T(8,128)S(1)}, f32[64,512]{1,0:T(8,128)S(1)}, f32...) custom-call(bf16[8,32,512]{2,1,0:T(8,128)(2,1)} %refs_0_.1, ...), custom_call_target="tpu_custom_call" | custom-call | tf_op jit(solution)/shard_map/layer/pallas_call | solution.py:995
  59.3 1.1 %place.1 = (bf16[8,32,512]{2,1,0:T(8,128)(2,1)}, bf16[8,32,512]{2,1,0:T(8,128)(2,1)}, f32[256,128]{1,0:T(8,128)}, f32[64,512]{1,0:T(8,128)}, f32[64,128]{1,0:T(8...) custom-call(bf16[8,32,512]{2,1,0:T(8,128)(2,1)S(1)} %get-tuple-eleme, ...), custom_call_target="tpu_custom_call" | custom-call | tf_op jit(solution)/shard_map/place/pallas_call | solution.py:1021

commit v5 on v4

--- a/solution.py
+++ b/solution.py
@@ -17,10 +17,10 @@
 LANES = 128
 ORDER = (
     "f10", "f13", "f11", "g10", "g11", "dnc", "f12", "g12", "g13", "dnb", "f21", "dnc", "Abar", "dna", "f20",
-    "dnb", "dna", "upa", "f23", "f22", "lo", "upb", "upa", "Alo", "ln2b", "dmix", "outg", "ab3", "upb",
+    "dnb", "upa", "f23", "dna", "f22", "lo", "upb", "upa", "Alo", "ln2b", "dmix", "ab3", "outg", "upb",
     "outa", "ab0", "outa", "ab2", "ab1", "dnc", "dnb", "bar", "dnq", "qkvg", "dsend", "pb", "pb", "pa", "upa",
-    "pa", "outa", "upb", "dnb", "Wd", "ln1b", "vec", "Aig", "dnb", "upa", "vec", "dna", "pb", "upb", "outa",
-    "pa", "dnc", "vec", "pb", "dna", "pa", "vec", "upa", "pb", "outa", "dna", "dnb", "dnc", "upb", "pa",
+    "pa", "outa", "upb", "dnb", "Wd", "ln1b", "Aig", "vec", "dnb", "upa", "vec", "dna", "pb", "upb", "outa",
+    "pa", "vec", "pb", "dnc", "dna", "pa", "vec", "upa", "pb", "dna", "dnb", "dnc", "upb", "outa", "pa",
     "dna", "dnc", "pb", "upa", "vec", "outa", "pa",
 )
 STAGES = {
@@ -122,6 +122,7 @@
         }
         seqs, heads = list(range(self.seq_bits)), list(range(self.seq_bits, self.bits))
         ways = {"core": seqs[:1], "straight": seqs[1:], "back": seqs[:0:-1], "bits": heads, "head": ["head"]}
+        ways["quad"] = ["quad"] if len(seqs) == 3 else seqs[1:]
         stages = {name: [b for way in ("core",) + STAGES[name] for b in ways[way]] for name in STAGES}
         rows_down, rows_up, rows_out = hidden // seq, width // seq, width // seq
         self.fine = rows_down % (2 * LANES) == 0
@@ -166,14 +167,18 @@
     def sum_shape(self, name):
         return (sum(part[2] - part[1] for part in self.sums[name][0]), LANES)
 
+    def bits_of(self, stage):
+        if stage == "head":
+            return list(range(self.seq_bits, self.bits))
+        return list(range(1, self.seq_bits)) if stage == "quad" else [stage]
+
     def got_shapes(self, name):
         left, shapes = self.bits, []
-        for b in self.sums[name][1]:
-            if b == "head":
-                shapes.append((self.head - 1,) + self.sum_shape(name))
-            else:
-                left -= 1
-                shapes.append((2,) * left + self.sum_shape(name))
+        for stage in self.sums[name][1]:
+            settled = len(self.bits_of(stage))
+            left -= settled
+            many = (2**settled - 1,) if isinstance(stage, str) else ()
+            shapes.append(many + (2,) * left + self.sum_shape(name))
         return shapes
 
 
@@ -190,11 +195,11 @@
         n = self.plan.seq_bits
         return bit_of(self.s, b) if b < n else bit_of(self.h, b - n)
 
-    def index(self, fixed, other=None):
+    def index(self, fixed, others={}):
         at = []
         for b in reversed(range(self.plan.bits)):
-            if b == other:
-                at.append(1 - self.own_bit(b))
+            if b in others:
+                at.append(others[b])
             elif b in fixed:
                 at.append(self.own_bit(b))
             else:
@@ -222,39 +227,45 @@
         )
         copy.start()
         self.started.append(copy)
+        return copy
+
+    def settled(self, stage):
+        return [b for way in self.order[:stage] for b in self.plan.bits_of(way)]
 
     def start(self, stage):
-        b = self.order[stage]
-        n = self.plan.seq_bits
-        if b == "head":
-            for k in range(1, self.plan.head):
-                peer = flip(self.h, k)
-                at = tuple(bit_of(peer, i) for i in reversed(range(self.plan.head_bits)))
-                at += self.index(range(n))[self.plan.head_bits :]
-                self.copy(self.grad.at[at], self.got[stage].at[k - 1], stage + k - 1, (self.s, peer))
+        way = self.order[stage]
+        n, first = self.plan.seq_bits, len(self.started)
+        self.arriving = []
+        if isinstance(way, str):
+            bits = self.plan.bits_of(way)
+            base = 1 << bits[0] if way == "quad" else 1
+            for k in range(1, 2 ** len(bits)):
+                device = (flip(self.s, k * base), self.h) if way == "quad" else (self.s, flip(self.h, k))
+                others = {b: bit_of(device[0], b) if b < n else bit_of(device[1], b - n) for b in bits}
+                source = self.grad.at[self.index(self.settled(stage), others)]
+                self.arriving.append(self.copy(source, self.got[stage].at[k - 1], first + k - 1, device))
             return
+        b = way
         device = (flip(self.s, 1 << b), self.h) if b < n else (self.s, flip(self.h, 1 << (b - n)))
-        source = self.grad.at[self.index(self.order[:stage], b)]
-        self.copy(source, self.got[stage], stage, device)
+        source = self.grad.at[self.index(self.settled(stage), {b: 1 - self.own_bit(b)})]
+        self.arriving.append(self.copy(source, self.got[stage], first, device))
 
     def finish(self, stage):
-        b = self.order[stage]
+        arriving = self.arriving
+        for copy in arriving:
+            copy.wait_recv()
+        got = self.got[stage]
+        pieces = [got.at[k] for k in range(len(arriving))] if len(arriving) > 1 else [got]
+        at = self.index(self.settled(stage + 1))
         if stage + 1 == len(self.order):
-            total = self.grad[self.index(range(self.plan.bits))].astype(F32)
-            if b == "head":
-                for k in range(1, self.plan.head):
-                    self.started[stage + k - 1].wait_recv()
-                    total = total + self.got[stage][k - 1].astype(F32)
-            else:
-                self.started[stage].wait_recv()
-                total = total + self.got[stage][...].astype(F32)
+            total = self.grad[at].astype(F32)
+            for piece in pieces:
+                total = total + piece[...].astype(F32)
             first = 0
             for part, r0, r1, c0, c1 in self.parts:
                 self.outs[part][r0:r1, c0:c1] = total[first : first + r1 - r0]
                 first += r1 - r0
             return
-        self.started[stage].wait_recv()
-        at = self.index(self.order[: stage + 1])
         combos = [()]
         for a in at:
             if isinstance(a, slice):
@@ -262,7 +273,13 @@
         for combo in combos:
             left = list(combo)
             full = tuple(left.pop(0) if isinstance(a, slice) else a for a in at)
-            self.grad[full] = self.grad[full] + self.got[stage][combo]
+            if len(pieces) == 1:
+                self.grad[full] = self.grad[full] + pieces[0][combo]
+                continue
+            total = self.grad[full].astype(F32)
+            for piece in pieces:
+                total = total + piece[combo].astype(F32)
+            self.grad[full] = total.astype(BF)
 
     def step(self):
         if self.stage:
@@ -296,7 +313,7 @@
     xg, dyg, log, igg = take(4)
     wq, wk, wv, wo, wu, wd = weights = take(6)
     gain_one, shift_one, gain_two, shift_two, up_bias, down_bias = lines = take(6)
-    norm_t, n_one, rs_one, n_two, rs_two, norm_two_b, residual, d_residual = take(8)
+    norm_t, norm_b, n_one, rs_one, n_two, rs_two, norm_two_b, residual, d_residual = take(9)
     qs, kn, vn, kf, vf, near_values = take(6)
     pn, pf, stats, mask, mixed_t = take(5)
     act_ref, hid_ref, cdf_ref, dh_ref = take(4)
@@ -455,18 +472,19 @@
 
     loads[0].wait()
     stack_heads(qs, (dot(normed, wq[...]) * (DH**-0.5)).astype(BF))
-    norm_t[...] = turned(normed)
+    norm_b[...] = normed
 
     def attend_near(p):
+        scores = jnp.concatenate([dot_t(kn[p, a], qs[p, a]) + mask[...] for a in range(2)], axis=1)
+        top = jnp.max(scores, axis=0, keepdims=True)
+        raised = jnp.exp(scores - top)
+        at = slice(2 * p * tokens, (2 * p + 2) * tokens)
+        stats[0:1, at] = top
+        stats[1:2, at] = jnp.sum(raised, axis=0, keepdims=True)
         for a in range(2):
-            at = slice((2 * p + a) * tokens, (2 * p + a + 1) * tokens)
-            scores = dot_t(kn[p, a], qs[p, a]) + mask[...]
-            top = jnp.max(scores, axis=0, keepdims=True)
-            raised = jnp.exp(scores - top)
-            pn[p, a] = raised
-            stats[0:1, at] = top
-            stats[1:2, at] = jnp.sum(raised, axis=0, keepdims=True)
-            near_values[p, a] = dot(turned(vn[p, a]), raised.astype(BF))
+            part = raised[:, a * tokens : (a + 1) * tokens]
+            pn[p, a] = part
+            near_values[p, a] = t_dot(vn[p, a], part.astype(BF))
 
     for p in range(plan.pairs):
         attend_near(p)
@@ -781,7 +799,7 @@
         i_a = lax.broadcasted_iota(jnp.int32, (BLOCK, tokens), 0)
         i_b = lax.broadcasted_iota(jnp.int32, (BLOCK, tokens), 1)
         mean_all = jnp.where((i_b >> plan.local) == i_a, 0.5**plan.local, 0.0).astype(BF)
-        bar_send[...] = dot_t(mean_all, norm_t[...]).astype(BF)
+        bar_send[...] = dot(mean_all, norm_b[...]).astype(BF)
         for k in range(1, plan.groups):
             other, device = row_peer(k)
             copy = pltpu.make_async_remote_copy(
@@ -796,6 +814,7 @@
             bar_copies.append(copy)
 
     def take_bars():
+        norm_t[...] = turned(norm_b[...])
         for copy in bar_copies:
             copy.wait_recv()
         for b in range(plan.remote):
@@ -927,6 +946,7 @@
     scratch += [buf(1, n, dtype=F32) for n in (width, width, width, width, hidden, width)]
     scratch += [
         buf(width, tokens),
+        buf(tokens, width),
         buf(tokens, width, dtype=F32),
         buf(tokens, 1, dtype=F32),
         buf(tokens, width, dtype=F32),

time: 60.7 us -> 60.3 us (level)
  no operation moved by 1% of the time
where the time goes in v5:
time: 60.3 us; the launch traced here: 60.1 us
  Pallas kernels  59.3 us (98%)
  between operations  0.82 us (1%)
    pallas_call x1, Pallas kernels, body(): pl.pallas_call(functools.partial(layer_kernel, plan), out_shape=[pltpu.VM...  58.3 us

profile of v5, /device:TPU:0, one launch (start us, length us, event | category | flops | bytes accessed | tf_op | source)
XLA Modules:
  0.0 60.1 jit_solution(13242494191429417022)
XLA Ops:
  0.7 58.3 %layer.1 = (bf16[8,32,512]{2,1,0:T(8,128)(2,1)S(1)}, bf16[8,32,512]{2,1,0:T(8,128)(2,1)S(1)}, f32[256,128]{1,0:T(8,128)S(1)}, f32[64,512]{1,0:T(8,128)S(1)}, f32...) custom-call(bf16[8,32,512]{2,1,0:T(8,128)(2,1)} %refs_0_.1, ...), custom_call_target="tpu_custom_call" | custom-call | tf_op jit(solution)/shard_map/layer/pallas_call | solution.py:1015
  58.9 1.1 %place.1 = (bf16[8,32,512]{2,1,0:T(8,128)(2,1)}, bf16[8,32,512]{2,1,0:T(8,128)(2,1)}, f32[256,128]{1,0:T(8,128)}, f32[64,512]{1,0:T(8,128)}, f32[64,128]{1,0:T(8...) custom-call(bf16[8,32,512]{2,1,0:T(8,128)(2,1)S(1)} %get-tuple-eleme, ...), custom_call_target="tpu_custom_call" | custom-call | tf_op jit(solution)/shard_map/place/pallas_call | solution.py:1041

commit v6 on v5

--- a/solution.py
+++ b/solution.py
@@ -457,7 +457,7 @@
     c_half[: BLOCK // 2, :] = level[:, :width]
     c_half[BLOCK // 2 :, :] = level[:, width:]
     c_copies = []
-    for k in range(1, plan.groups):
+    for k in reversed(range(1, plan.groups)):
         other, device = row_peer(k)
         copy = pltpu.make_async_remote_copy(
             src_ref=c_send if k == 1 else c_half,

time: 60.3 us -> 60.3 us (level)
  no operation moved by 1% of the time
where the time goes in v6:
time: 60.3 us; the launch traced here: 60.2 us
  Pallas kernels  59.3 us (98%)
  between operations  0.82 us (1%)
    pallas_call x1, Pallas kernels, body(): pl.pallas_call(functools.partial(layer_kernel, plan), out_shape=[pltpu.VM...  58.3 us

profile of v6, /device:TPU:0, one launch (start us, length us, event | category | flops | bytes accessed | tf_op | source)
XLA Modules:
  0.0 60.2 jit_solution(15767322310670311098)
XLA Ops:
  0.7 58.3 %layer.1 = (bf16[8,32,512]{2,1,0:T(8,128)(2,1)S(1)}, bf16[8,32,512]{2,1,0:T(8,128)(2,1)S(1)}, f32[256,128]{1,0:T(8,128)S(1)}, f32[64,512]{1,0:T(8,128)S(1)}, f32...) custom-call(bf16[8,32,512]{2,1,0:T(8,128)(2,1)} %refs_0_.1, ...), custom_call_target="tpu_custom_call" | custom-call | tf_op jit(solution)/shard_map/layer/pallas_call | solution.py:1015
  58.9 1.1 %place.1 = (bf16[8,32,512]{2,1,0:T(8,128)(2,1)}, bf16[8,32,512]{2,1,0:T(8,128)(2,1)}, f32[256,128]{1,0:T(8,128)}, f32[64,512]{1,0:T(8,128)}, f32[64,128]{1,0:T(8...) custom-call(bf16[8,32,512]{2,1,0:T(8,128)(2,1)S(1)} %get-tuple-eleme, ...), custom_call_target="tpu_custom_call" | custom-call | tf_op jit(solution)/shard_map/place/pallas_call | solution.py:1041
